TPU v7x, 32 devices: a whole 2x2x4 slice. The times are simulated.
32 devices in a mesh: groups: 2 (over x), tm: 8 (over z, y), mp: 2 (over core).
Axes of the slice: x: 2, y: 2, z: 4, core: 2. Of those that a mesh axis runs over, the one named last changes fastest.
Arguments:
- frames: bfloat16 [8192, 1024], P(('groups', 'tm')), parts along dimension 0, may hold values from -6 to 6
- valid: int32 [8192], P(('groups', 'tm')), parts along dimension 0, may hold values from 0 to 1, as said below
- w_qkv: bfloat16 [1024, 3, 1024], P(None, None, 'mp'), may hold values from -1 to 1
- w_out: bfloat16 [1024, 1024], P('mp'), may hold values from -0.1875 to 0.1875
- gain_attn: float32 [1024], replicated, may hold values from 0.5 to 1.5
- w_conv_in: bfloat16 [1024, 2, 1024], P(None, None, 'mp'), may hold values from -0.1875 to 0.1875
- w_depth: float32 [9, 1024], P(None, 'mp'), may hold values from -2 to 2
- gain_conv: float32 [1024], replicated, may hold values from 0.5 to 1.5
- w_conv_out: bfloat16 [1024, 1024], P('mp'), may hold values from -0.1875 to 0.1875
- cotangent: bfloat16 [8192, 1024], P(('groups', 'tm')), parts along dimension 0, may hold values from -6 to 6
Outputs:
- output: bfloat16 [8192, 1024], P(('groups', 'tm')), parts along dimension 0
- grad_frames: bfloat16 [8192, 1024], P(('groups', 'tm')), parts along dimension 0
- grad_qkv: float32 [2048, 3, 1024], P(('groups', 'tm'), None, 'mp'), parts along dimension 0
- grad_proj: float32 [2048, 1024], P(('groups', 'mp'), 'tm'), parts along dimension 0
- grad_gain_attn: float32 [2048], P(('groups', 'tm')), parts along dimension 0
- grad_conv_in: float32 [2048, 2, 1024], P(('groups', 'tm'), None, 'mp'), parts along dimension 0
- grad_depth: float32 [18, 1024], P('groups', ('mp', 'tm')), parts along dimension 0
- grad_conv_out: float32 [2048, 1024], P(('groups', 'mp'), 'tm'), parts along dimension 0
- grad_gain_conv: float32 [2048], P(('groups', 'tm')), parts along dimension 0
There are 2 independent parts, one for each index of `groups`. A program takes and returns all parts, laid end to end along the dimension named above; an argument that names none is the same for every part. Nothing has to cross between parts.
Inputs may be any that keep to these rules, and one draw needn't show every extreme that they name: `valid`: 1 on the frames of the recording, which begin at frame 0, and 0 on the padding after it; the first half of the 4096 frames are always 1 and the last frame is always 0.
All inputs are finite; a program needn't handle non-finite values.
Results may differ from a plain program's by a relative error of at most 0.018.
Values may be sent and summed in bfloat16 or wider, within the bound.
No kernel may reach another device: no remote copies, remote signals or barrier semaphores. Data moves between devices by JAX's collectives and lax.ppermute only.
A program may use at most 128 MiB of HBM per device.

v0:
```python
import jax
import jax.numpy as jnp
from jax import lax
from jax.sharding import PartitionSpec as P

HEAD_DIM = 128
KERNEL = 9
REACH = 128


epsilon = 1e-05
query_block = 512


def extended(array, sides, width):
    for axis, dim in sides:
        devices, length = (lax.axis_size(axis), array.shape[dim])
        up = [(i, (i + 1) % devices) for i in range(devices - 1)]
        down = [(j, i) for i, j in up]
        last = lax.slice_in_dim(array, length - width, length, axis=dim)
        initial = lax.slice_in_dim(array, 0, width, axis=dim)
        before = lax.ppermute(last, axis, up)
        after = lax.ppermute(initial, axis, down)
        array = jnp.concatenate([before, array, after], axis=dim)
    return array


def normalize(values, gain):
    center = jnp.mean(values, axis=-1, keepdims=True)
    centred = values - center
    inverse = lax.rsqrt(jnp.mean(centred * centred, axis=-1, keepdims=True) + epsilon)
    normed = centred * inverse
    return (normed * gain, normed, inverse)


def normalize_back(upstream, gain, normed, inverse):
    scaled = upstream * gain
    first_mean = jnp.mean(scaled, axis=-1, keepdims=True)
    second_mean = jnp.mean(scaled * normed, axis=-1, keepdims=True)
    return (
        inverse * (scaled - first_mean - normed * second_mean),
        jnp.sum(upstream * normed, axis=0),
    )


def attention_weights(queries, key_block, key_valid, reach_rows, score_scale):
    scores = (
        jnp.einsum("qhd,khd->hqk", queries, key_block, preferred_element_type=jnp.float32)
        * score_scale
    )
    grid_shape = (queries.shape[0], key_block.shape[0])
    offset = (
        lax.broadcasted_iota(jnp.int32, grid_shape, 1)
        - lax.broadcasted_iota(jnp.int32, grid_shape, 0)
        - reach_rows
    )
    allowed = (jnp.abs(offset) <= reach_rows) & ((key_valid[None, :] > 0) | (offset == 0))
    masked = jnp.where(allowed[None], scores, -jnp.inf)
    highest = jnp.max(masked, axis=-1, keepdims=True)
    raised = jnp.exp(masked - highest)
    return raised / jnp.sum(raised, axis=-1, keepdims=True)


def model_sum(partial_sum):
    return lax.psum(partial_sum, "mp")


def conv_edges(signal):
    return extended(signal, (("tm", 0),), (KERNEL - 1) // 2)


def local(
    frames, valid, w_qkv, w_out, gain_attn, w_conv_in, w_depth, gain_conv, w_conv_out, cotangent
):
    frame_rows, model_width = frames.shape
    local_width = w_out.shape[0]
    head_count = local_width // HEAD_DIM
    reach_rows = REACH
    half_kernel = (KERNEL - 1) // 2
    block_rows = min(frame_rows, query_block)
    window_rows = block_rows + 2 * reach_rows
    score_scale = HEAD_DIM ** (-0.5)
    bf16 = jnp.bfloat16
    f32 = jnp.float32
    contract_rows = (((0,), (0,)), ((), ()))
    contract_cols = (((1,), (1,)), ((), ()))
    frame_mask = valid.astype(f32)
    source = frames.astype(f32)
    gained_attn, normed_attn, inverse_attn = normalize(source, gain_attn)
    attn_in = gained_attn.astype(bf16)
    flat_qkv = w_qkv.reshape(model_width, 3 * local_width)
    projected = jnp.dot(attn_in, flat_qkv, preferred_element_type=f32).astype(bf16)
    projected = projected.reshape(frame_rows, 3, head_count, HEAD_DIM)
    queries = projected[:, 0]
    pair_pad, valid_pad = (
        extended(projected[:, 1:], (("tm", 0),), reach_rows),
        extended(frame_mask.astype(bf16), (("tm", 0),), reach_rows),
    )

    def block_inputs(block_index):
        first_row = block_index * block_rows
        weights = attention_weights(queries, pair_pad[:, 0], valid_pad, reach_rows, score_scale)
        return (first_row, queries, pair_pad, weights)

    block_index = 0
    first_row, query_rows, window, weights = block_inputs(block_index)
    attended_blocks = jnp.einsum(
        "hqk,khd->qhd", weights.astype(bf16), window[:, 1], preferred_element_type=f32
    ).astype(bf16)
    attended = attended_blocks.reshape(frame_rows, local_width)
    hidden = source + model_sum(jnp.dot(attended, w_out, preferred_element_type=f32))
    gained_conv, normed_conv, inverse_conv = normalize(hidden, gain_conv)
    conv_in = gained_conv.astype(bf16)
    flat_conv_in = w_conv_in.reshape(model_width, 2 * local_width)
    lifted = jnp.dot(conv_in, flat_conv_in, preferred_element_type=f32).reshape(
        frame_rows, 2, local_width
    )
    linear = lifted[:, 0]
    gate_sig = jax.nn.sigmoid(lifted[:, 1])
    gated = (linear * gate_sig * frame_mask[:, None]).astype(bf16)
    gated_pad = conv_edges(gated)
    depthwise = w_depth[0] * gated_pad[0:frame_rows]
    for tap_index in range(1, KERNEL):
        depthwise = depthwise + w_depth[tap_index] * gated_pad[tap_index : tap_index + frame_rows]
    acted = (depthwise * jax.nn.sigmoid(depthwise)).astype(bf16)
    output = (hidden + model_sum(jnp.dot(acted, w_conv_out, preferred_element_type=f32))).astype(
        bf16
    )
    conv_out_local = lax.dot_general(acted, cotangent, contract_rows, preferred_element_type=f32)
    grad_acted = lax.dot_general(
        cotangent, w_conv_out, contract_cols, preferred_element_type=f32
    ).astype(bf16)
    act_sig = jax.nn.sigmoid(depthwise)
    grad_depth_in = (grad_acted * (act_sig * (1.0 + depthwise * (1.0 - act_sig)))).astype(bf16)
    grad_depth_pad = conv_edges(grad_depth_in)
    depth_local = jnp.stack(
        [
            jnp.sum(
                grad_depth_in.astype(f32) * gated_pad[tap_index : tap_index + frame_rows], axis=0
            )
            for tap_index in range(KERNEL)
        ]
    )
    grad_gated = w_depth[0] * grad_depth_pad[2 * half_kernel : 2 * half_kernel + frame_rows]
    for tap_index in range(1, KERNEL):
        grad_gated = (
            grad_gated
            + w_depth[tap_index]
            * grad_depth_pad[2 * half_kernel - tap_index : 2 * half_kernel - tap_index + frame_rows]
        )
    grad_gated = grad_gated * frame_mask[:, None]
    grad_lifted = (
        jnp.stack(
            [grad_gated * gate_sig, grad_gated * linear * gate_sig * (1.0 - gate_sig)], axis=1
        )
        .astype(bf16)
        .reshape(frame_rows, 2 * local_width)
    )
    conv_in_local = lax.dot_general(
        conv_in, grad_lifted, contract_rows, preferred_element_type=f32
    ).reshape(model_width, 2, local_width)
    grad_norm_conv = model_sum(
        lax.dot_general(grad_lifted, flat_conv_in, contract_cols, preferred_element_type=f32)
    )
    back_conv, gain_conv_local = normalize_back(
        grad_norm_conv, gain_conv, normed_conv, inverse_conv
    )
    grad_hidden = cotangent.astype(f32) + back_conv
    hidden_grad_b = grad_hidden.astype(bf16)
    proj_local = lax.dot_general(attended, hidden_grad_b, contract_rows, preferred_element_type=f32)
    grad_attended = (
        lax.dot_general(hidden_grad_b, w_out, contract_cols, preferred_element_type=f32)
        .astype(bf16)
        .reshape(frame_rows, head_count, HEAD_DIM)
    )
    kv_grads = jnp.zeros((frame_rows + 2 * reach_rows, 2, head_count, HEAD_DIM), f32)
    block_index = 0
    first_row, query_rows, window, weights = block_inputs(block_index)
    grad_weights = jnp.einsum(
        "qhd,khd->hqk", grad_attended, window[:, 1], preferred_element_type=f32
    )
    spread_sum = jnp.sum(weights * grad_weights, axis=-1, keepdims=True)
    grad_scores = (weights * (grad_weights - spread_sum) * score_scale).astype(bf16)
    query_grads = jnp.einsum("hqk,khd->qhd", grad_scores, window[:, 0], preferred_element_type=f32)
    key_grad = jnp.einsum("hqk,qhd->khd", grad_scores, query_rows, preferred_element_type=f32)
    value_grad = jnp.einsum(
        "hqk,qhd->khd", weights.astype(bf16), grad_attended, preferred_element_type=f32
    )
    kv_grads = kv_grads.at[first_row : first_row + window_rows].add(
        jnp.stack([key_grad, value_grad], axis=1)
    )
    rim_grads = jnp.concatenate(
        [kv_grads[:reach_rows], kv_grads[frame_rows + reach_rows :]], axis=0
    )
    returned = extended(rim_grads.astype(jnp.bfloat16), (("tm", 0),), reach_rows).astype(
        rim_grads.dtype
    )
    own_grads = kv_grads[reach_rows : reach_rows + frame_rows]
    own_grads = own_grads.at[:reach_rows].add(returned[:reach_rows])
    own_grads = own_grads.at[frame_rows - reach_rows :].add(returned[3 * reach_rows :])
    query_block_grads = query_grads[:, None]
    grad_projected = (
        jnp.concatenate([query_block_grads, own_grads], axis=1)
        .astype(bf16)
        .reshape(frame_rows, 3 * local_width)
    )
    qkv_local = lax.dot_general(
        attn_in, grad_projected, contract_rows, preferred_element_type=f32
    ).reshape(model_width, 3, local_width)
    grad_norm_attn = model_sum(
        lax.dot_general(grad_projected, flat_qkv, contract_cols, preferred_element_type=f32)
    )
    back_attn, gain_attn_local = normalize_back(
        grad_norm_attn, gain_attn, normed_attn, inverse_attn
    )
    grad_frames = (grad_hidden + back_attn).astype(bf16)
    grad_qkv, grad_proj, grad_gain_attn, grad_conv_in, grad_depth, grad_conv_out, grad_gain_conv = (
        lax.psum_scatter(
            qkv_local.astype(jnp.bfloat16), "tm", scatter_dimension=0, tiled=True
        ).astype(jnp.float32),
        lax.psum_scatter(
            proj_local.astype(jnp.bfloat16), "tm", scatter_dimension=1, tiled=True
        ).astype(jnp.float32),
        lax.psum_scatter(
            gain_attn_local.astype(jnp.bfloat16), "tm", scatter_dimension=0, tiled=True
        ).astype(jnp.float32),
        lax.psum_scatter(
            conv_in_local.astype(jnp.bfloat16), "tm", scatter_dimension=0, tiled=True
        ).astype(jnp.float32),
        lax.psum_scatter(
            depth_local.astype(jnp.bfloat16), "tm", scatter_dimension=1, tiled=True
        ).astype(jnp.float32),
        lax.psum_scatter(
            conv_out_local.astype(jnp.bfloat16), "tm", scatter_dimension=1, tiled=True
        ).astype(jnp.float32),
        lax.psum_scatter(
            gain_conv_local.astype(jnp.bfloat16), "tm", scatter_dimension=0, tiled=True
        ).astype(jnp.float32),
    )
    return (
        output,
        grad_frames,
        grad_qkv,
        grad_proj,
        grad_gain_attn,
        grad_conv_in,
        grad_depth,
        grad_conv_out,
        grad_gain_conv,
    )


def solution(mesh):
    return jax.shard_map(
        local,
        mesh=mesh,
        in_specs=(
            P(("groups", "tm"), None),
            P(("groups", "tm")),
            P(None, None, "mp"),
            P("mp", None),
            P(),
            P(None, None, "mp"),
            P(None, "mp"),
            P(),
            P("mp", None),
            P(("groups", "tm"), None),
        ),
        out_specs=(
            P(("groups", "tm"), None),
            P(("groups", "tm"), None),
            P(("groups", "tm"), None, "mp"),
            P(("groups", "mp"), "tm"),
            P(("groups", "tm")),
            P(("groups", "tm"), None, "mp"),
            P("groups", ("mp", "tm")),
            P(("groups", "mp"), "tm"),
            P(("groups", "tm")),
        ),
        check_vma=False,
    )
```

profile of v0, /device:TPU:0, one launch (start us, length us, event | category | flops | bytes accessed | tf_op | source)
XLA Modules:
  0.0 522.7 jit_solution(3369878188280357383)
XLA Ops:
  7.2 1.5 convert_reduce_fusion
  8.8 1.6 fusion.29
  10.4 4.8 copy.47
  15.2 5.0 convolution_convert_fusion
  20.2 3.0 reshape.263
  23.4 4.9 collective-permute-start
  28.4 3.4 collective-permute-start.2
  31.8 1.3 collective-permute-start.3
  33.1 1.3 collective-permute-start.1
  35.0 2.2 collective-permute-done.3
  37.9 5.2 collective-permute-done.1
  44.2 2.9 fusion.129
  48.3 1.5 copy-done.34
  49.8 2.1 fusion.130
  52.1 2.2 copy.80
  54.3 2.6 copy.53
  56.9 17.9 %all-reduce.8.cloned.1.call-done = f32[512,1024]{1,0:T(8,128)} async-done(((f32[512,1024]{1,0:T(8,128)}), f32[512,1024]{1,0:T(8,128)}) %all-reduce.8.cloned.1.call-update) | async-done | bytes 2097168 | tf_op jit(solution)/shard_map/psum | solution.py:65
  74.8 2.1 fusion.121
  78.5 1.3 fusion.115
  80.2 3.6 collective-permute-start.4
  83.9 1.3 collective-permute-start.5
  85.2 4.2 collective-permute-done.5
  89.4 1.4 fusion.65
  90.8 2.5 fusion.81
  93.2 1.3 collective-permute-start.6
  94.5 4.9 collective-permute-start.7
  99.5 1.3 collective-permute-done.7
  100.8 2.3 multiply_bitcast_fusion.1
  105.0 2.6 fusion.33
  108.8 3.3 convolution_convert_fusion.3
  112.1 2.3 copy.74
  114.4 2.3 maximum_convert_fusion.1
  116.7 2.3 copy.59
  119.0 4.2 convolution_convert_fusion.2
  123.5 3.3 fusion.119
  126.8 5.5 %all-reduce.10.cloned.1.call-done = f32[512,1024]{1,0:T(8,128)} async-done(((f32[512,1024]{1,0:T(8,128)}), f32[512,1024]{1,0:T(8,128)}) %all-reduce.10.cloned.1.call-update) | async-done | bytes 2097168 | tf_op jit(solution)/shard_map/psum | solution.py:65
  132.3 2.6 multiply_reduce_fusion.1
  135.7 1.3 copy-done.2
  137.0 1.7 convolution_convert_fusion.4
  138.7 2.3 copy.70
  141.0 2.3 convolution_convert_fusion.5
  143.3 5.0 fusion.43
  148.4 5.0 fusion.88
  153.4 18.0 %fusion.46 = f32[768,1,4,128]{0,3,2,1:T(8,128)} fusion(f32[4,512,768]{2,1,0:T(8,128)} %fusion.88, bf16[512,1,4,128]{3,2,1,0:T(4,128)(2,1)S(1)} %copy-done.23, f32[4,512,768]{2,1,0:T(8,128)} %copy-done.34, f32[4,512]{1,0:T(4,128)S(1)} %get-tuple-element.128), kind=kOutput, calls=%fused_computation.75 | convolution fusion | flops 413666048 | bytes 14688256 | tf_op jit(solution)/shard_map/hqk,qhd->khd/dot_general | solution.py:185
  171.4 2.3 fusion.6
  173.9 3.7 collective-permute-start.8
  178.9 1.6 fusion.30
  180.5 18.2 %fusion.49 = bf16[512,1,4,128]{0,3,2,1:T(8,128)(2,1)} fusion(f32[4,512,768]{2,1,0:T(8,128)} %fusion.88, bf16[768,2,4,128]{3,0,2,1:T(8,128)(2,1)} %copy-done.14, f32[4,512,768]{2,1,0:T(8,128)} %copy-done.34, f32[4,512]{1,0:T(4,128)S(1)} %get-tuple-element.128), kind=kOutput, calls=%fused_computation.78 | convolution fusion | flops 413666048 | bytes 26492928 | tf_op jit(solution)/shard_map/hqk,khd->qhd/dot_general | solution.py:184
  198.7 1.9 fusion.104
  200.6 2.0 fusion.105
  202.6 1.9 maximum_convert_fusion
  205.7 3.2 fusion.131
  210.1 5.2 convolution_convert_fusion.1
  218.6 47.3 %reduce-scatter.20.cloned.1.call-done = bf16[128,512]{1,0:T(8,128)(2,1)} async-done(((bf16[1024,512]{1,0:T(8,128)(2,1)}), bf16[128,512]{1,0:T(8,128)(2,1)}) %reduce-scatter.20.cloned.1.call-update) | async-done | bytes 131088
  267.6 69.0 %reduce-scatter.14.cloned.1.call-done = bf16[128,2,512]{2,0,1:T(8,128)(2,1)} async-done(((bf16[1024,2,512]{2,0,1:T(8,128)(2,1)}), bf16[128,2,512]{2,0,1:T(8,128)(2,1)}) %reduce-scatter.14.cloned.1.call-update) | async-done | bytes 262160 | tf_op jit(solution)/shard_map/reduce_scatter | solution.py:227
  336.7 2.0 copy.61
  338.7 65.2 %reduce-scatter.16.cloned.1.call-done = bf16[128,512]{1,0:T(8,128)(2,1)} async-done(((bf16[1024,512]{1,0:T(8,128)(2,1)}), bf16[128,512]{1,0:T(8,128)(2,1)}) %reduce-scatter.16.cloned.1.call-update) | async-done | bytes 131088
  405.6 28.1 %all-reduce.12.cloned.1.call-done = (f32[512,1024]{1,0:T(8,128)}, f32[512,1024]{1,0:T(8,128)}) async-done(((f32[512,1024]{1,0:T(8,128)}, f32[512,1024]{1,0:T(8,128)}), (f32[512,1024]{1,0:T(8,128)}, f32[512,1024]{1,0:T(8,128)})) %all-reduce.12.cloned.1.call-update) | async-done | bytes 4194320 | tf_op jit(solution)/shard_map/psum | solution.py:65
  433.7 2.5 fusion.28
  436.2 22.0 %all-reduce.3 = (bf16[1024]{0:T(1024)(128)(2,1)S(1)}, bf16[1024]{0:T(1024)(128)(2,1)S(1)}) all-reduce(bf16[1024]{0:T(1024)(128)(2,1)S(1)} %get-tuple-element.82, bf16[1024]{0:T(1024)(128)(2,1)S(1)} %get-tuple-element.80), channel_id=4, replica_groups=mesh['groups'=2,'tm'=8,'mp'=2] {'tm'}, use_global_device_ids=true, to_apply=%region_18.19.clone | all-reduce | flops 2048 | bytes 8192
  459.3 3.1 add_convert_fusion
  463.1 1.7 fusion.27
  464.8 48.6 %reduce-scatter.12.cloned.1.call-done = bf16[128,3,512]{2,0,1:T(8,128)(2,1)} async-done(((bf16[1024,3,512]{2,0,1:T(8,128)(2,1)}), bf16[128,3,512]{2,0,1:T(8,128)(2,1)}) %reduce-scatter.12.cloned.1.call-update) | async-done | bytes 393232 | tf_op jit(solution)/shard_map/reduce_scatter | solution.py:218
  513.4 2.0 convert_element_type.241
  (141 shorter events, 21.8 us)
Async XLA Ops:
  7.2 83.6 %copy-start = (bf16[512,1024]{1,0:T(8,128)(2,1)S(1)}, bf16[512,1024]{1,0:T(8,128)(2,1)}, u32[]{:S(2)}) copy-start(bf16[512,1024]{1,0:T(8,128)(2,1)} %param.26) | copy-start | bytes 3145732
  7.2 67.6 %all-reduce.8.cloned.1.call-start = ((), (), s32[]{:S(2)}) async-start(), calls=%async_computation.5 | async-start | bytes 4194304 | tf_op jit(solution)/shard_map/psum | solution.py:65
  10.4 4.8 copy-start.4
  10.4 4.8 copy-start.30
  20.2 8.1 %copy-start.32 = (s32[512]{0:T(512)S(1)}, s32[512]{0:T(512)}, u32[]{:S(2)}) copy-start(s32[512]{0:T(512)} %param.19) | copy-start | bytes 6148
  23.4 14.2 %collective-permute-start = (bf16[128,2,4,128]{3,0,2,1:T(8,128)(2,1)S(1)}, bf16[128,2,4,128]{3,0,2,1:T(8,128)(2,1)S(1)}, u32[]{:S(2)}, u32[]{:S(2)}) collective-permute-start(bf16[128,2,4,128]{3,0,2,1:T(8,128)(2,1)S(1)} %copy.76), channel_id=1, source_target_pairs={{0,2},{2,4},{4,6},{6,8},{8,10},{10,12},{12,14},{1,3},{3,5},{5,7},{... | collective-permute-start | bytes 786440 | tf_op jit(solution)/shard_map/ppermute | solution.py:22
  28.4 6.6 %collective-permute-start.2 = (bf16[128]{0:T(256)(128)(2,1)S(1)}, bf16[128]{0:T(256)(128)(2,1)S(1)}, u32[]{:S(2)}, u32[]{:S(2)}) collective-permute-start(bf16[128]{0:T(256)(128)(2,1)S(1)} %get-tuple-element.126), channel_id=1, source_target_pairs={{0,2},{2,4},{4,6},{6,8},{8,10},{10,12},{12,14},{1,3},{3,5},{5,7},{... | collective-permute-start | bytes 776 | tf_op jit(solution)/shard_map/ppermute | solution.py:22
  31.8 5.5 %collective-permute-start.3 = (bf16[128]{0:T(256)(128)(2,1)S(1)}, bf16[128]{0:T(256)(128)(2,1)S(1)}, u32[]{:S(2)}, u32[]{:S(2)}) collective-permute-start(bf16[128]{0:T(256)(128)(2,1)S(1)} %get-tuple-element.127), channel_id=1, source_target_pairs={{2,0},{4,2},{6,4},{8,6},{10,8},{12,10},{14,12},{3,1},{5,3},{7,5},{... | collective-permute-start | bytes 776 | tf_op jit(solution)/shard_map/ppermute | solution.py:23
  33.1 10.0 %collective-permute-start.1 = (bf16[128,2,4,128]{3,0,2,1:T(8,128)(2,1)S(1)}, bf16[128,2,4,128]{3,0,2,1:T(8,128)(2,1)S(1)}, u32[]{:S(2)}, u32[]{:S(2)}) collective-permute-start(bf16[128,2,4,128]{3,0,2,1:T(8,128)(2,1)S(1)} %copy.78), channel_id=1, source_target_pairs={{2,0},{4,2},{6,4},{8,6},{10,8},{12,10},{14,12},{3,1},{5,3},{7,5},{... | collective-permute-start | bytes 786440 | tf_op jit(solution)/shard_map/ppermute | solution.py:23
  35.0 9.2 %copy-start.22 = (bf16[512,1,4,128]{3,2,1,0:T(4,128)(2,1)}, bf16[512,1,4,128]{3,2,1,0:T(4,128)(2,1)S(1)}, u32[]{:S(2)}) copy-start(bf16[512,1,4,128]{3,2,1,0:T(4,128)(2,1)S(1)} %slice.308) | copy-start | bytes 1572868
  43.2 3.9 copy-start.14
  47.1 2.7 copy-start.34
  47.1 2.6 copy-start.11
  49.8 2.1 copy-start.15
  51.9 80.3 %all-reduce.10.cloned.1.call-start = ((), (), s32[]{:S(2)}) async-start(), calls=%async_computation.6 | async-start | bytes 4194304 | tf_op jit(solution)/shard_map/psum | solution.py:65
  76.9 1.6 copy-start.18
  76.9 1.6 copy-start.29
  79.9 5.3 %copy-start.31 = (f32[9,512]{1,0:T(8,128)S(1)}, f32[9,512]{1,0:T(8,128)}, u32[]{:S(2)}) copy-start(f32[9,512]{1,0:T(8,128)} %param.24) | copy-start | bytes 55300
  79.9 10.9 %copy-start.26 = (bf16[512,1024]{1,0:T(8,128)(2,1)S(1)}, bf16[512,1024]{1,0:T(8,128)(2,1)}, u32[]{:S(2)}) copy-start(bf16[512,1024]{1,0:T(8,128)(2,1)} %param.27) | copy-start | bytes 3145732
  80.2 5.0 collective-permute-start.4
  83.9 5.5 %collective-permute-start.5 = (bf16[4,512]{1,0:T(4,128)(2,1)S(1)}, bf16[4,512]{1,0:T(4,128)(2,1)S(1)}, u32[]{:S(2)}, u32[]{:S(2)}) collective-permute-start(bf16[4,512]{1,0:T(4,128)(2,1)S(1)} %get-tuple-element.114), channel_id=1, source_target_pairs={{2,0},{4,2},{6,4},{8,6},{10,8},{12,10},{14,12},{3,1},{5,3},{7,5},{... | collective-permute-start | bytes 12296 | tf_op jit(solution)/shard_map/ppermute | solution.py:23
  90.7 2.5 copy-start.25
  93.2 6.2 %collective-permute-start.6 = (bf16[4,512]{1,0:T(4,128)(2,1)S(1)}, bf16[4,512]{1,0:T(4,128)(2,1)S(1)}, u32[]{:S(2)}, u32[]{:S(2)}) collective-permute-start(bf16[4,512]{1,0:T(4,128)(2,1)S(1)} %get-tuple-element.111), channel_id=1, source_target_pairs={{2,0},{4,2},{6,4},{8,6},{10,8},{12,10},{14,12},{3,1},{5,3},{7,5},{... | collective-permute-start | bytes 12296 | tf_op jit(solution)/shard_map/ppermute | solution.py:23
  94.5 6.2 %collective-permute-start.7 = (bf16[4,512]{1,0:T(4,128)(2,1)S(1)}, bf16[4,512]{1,0:T(4,128)(2,1)S(1)}, u32[]{:S(2)}, u32[]{:S(2)}) collective-permute-start(bf16[4,512]{1,0:T(4,128)(2,1)S(1)} %get-tuple-element.112), channel_id=1, source_target_pairs={{0,2},{2,4},{4,6},{6,8},{8,10},{10,12},{12,14},{1,3},{3,5},{5,7},{... | collective-permute-start | bytes 12296 | tf_op jit(solution)/shard_map/ppermute | solution.py:22
  103.0 0.8 copy-start.19
  103.1 2.0 copy-start.17
  103.5 0.8 copy-start.20
  107.7 109.5 %reduce-scatter.18.cloned.1.call-start = ((), (), s32[]{:S(2)}) async-start(), calls=%async_computation.10 | async-start | bytes 147456
  108.7 157.2 %reduce-scatter.20.cloned.1.call-start = ((), (), s32[]{:S(2)}) async-start(), calls=%async_computation.11 | async-start | bytes 1179648
  114.4 222.3 %reduce-scatter.14.cloned.1.call-start = ((), (), s32[]{:S(2)}) async-start(), calls=%async_computation.8 | async-start | bytes 2359296 | tf_op jit(solution)/shard_map/reduce_scatter | solution.py:227
  123.2 280.6 %reduce-scatter.16.cloned.1.call-start = ((), (), s32[]{:S(2)}) async-start(), calls=%async_computation.9 | async-start | bytes 1179648
  126.8 8.1 %copy-start.27 = (bf16[512,1024]{1,0:T(8,128)(2,1)S(1)}, bf16[512,1024]{1,0:T(8,128)(2,1)}, u32[]{:S(2)}) copy-start(bf16[512,1024]{1,0:T(8,128)(2,1)} %param.27) | copy-start | bytes 3145732
  132.3 2.6 copy-start.10
  134.9 2.2 copy-start.16
  135.7 1.4 copy-start.2
  137.0 4.0 copy-start.12
  143.3 5.0 copy-start.21
  148.3 5.1 copy-start.23
  148.3 285.4 %all-reduce.12.cloned.1.call-start = ((), (), s32[]{:S(2)}) async-start(), calls=%async_computation.12 | async-start | bytes 8388608 | tf_op jit(solution)/shard_map/psum | solution.py:65
  171.4 7.4 %copy-start.7 = (f32[768,1,4,128]{0,3,2,1:T(8,128)S(1)}, f32[768,1,4,128]{0,3,2,1:T(8,128)}, u32[]{:S(2)}) copy-start(f32[768,1,4,128]{0,3,2,1:T(8,128)} %fusion.43) | copy-start | bytes 4718596
  171.4 7.4 %copy-start.8 = (f32[768,1,4,128]{0,3,2,1:T(8,128)S(1)}, f32[768,1,4,128]{0,3,2,1:T(8,128)}, u32[]{:S(2)}) copy-start(f32[768,1,4,128]{0,3,2,1:T(8,128)} %fusion.46) | copy-start | bytes 4718596
  173.9 24.8 %collective-permute-start.8 = (bf16[128,2,4,128]{0,3,2,1:T(8,128)(2,1)S(1)}, bf16[128,2,4,128]{0,3,2,1:T(8,128)(2,1)S(1)}, u32[]{:S(2)}, u32[]{:S(2)}) collective-permute-start(bf16[128,2,4,128]{0,3,2,1:T(8,128)(2,1)S(1)} %get-tuple-element.107), channel_id=1, source_target_pairs={{0,2},{2,4},{4,6},{6,8},{8,10},{10,12},{12,14},{1,3},{3,5},{5,7},{... | collective-permute-start | bytes 786440 | tf_op jit(solution)/shard_map/ppermute | solution.py:22
  177.5 21.1 %collective-permute-start.9 = (bf16[128,2,4,128]{0,3,2,1:T(8,128)(2,1)S(1)}, bf16[128,2,4,128]{0,3,2,1:T(8,128)(2,1)S(1)}, u32[]{:S(2)}, u32[]{:S(2)}) collective-permute-start(bf16[128,2,4,128]{0,3,2,1:T(8,128)(2,1)S(1)} %get-tuple-element.108), channel_id=1, source_target_pairs={{2,0},{4,2},{6,4},{8,6},{10,8},{12,10},{14,12},{3,1},{5,3},{7,5},{... | collective-permute-start | bytes 786440 | tf_op jit(solution)/shard_map/ppermute | solution.py:23
  200.6 2.0 copy-start.28
  202.6 3.1 copy-start.13
  204.5 1.2 copy-start.24
  208.9 1.2 copy-start.5
  208.9 304.5 %reduce-scatter.12.cloned.1.call-start = ((), (), s32[]{:S(2)}) async-start(), calls=%async_computation.7 | async-start | bytes 3538944 | tf_op jit(solution)/shard_map/reduce_scatter | solution.py:218
  215.3 0.7 copy-start.33
  459.3 3.1 copy-start.3
  459.3 3.1 copy-start.6
  459.3 3.7 copy-start.9
  463.1 52.3 %copy-start.1 = (bf16[512,1024]{1,0:T(8,128)(2,1)S(1)}, bf16[512,1024]{1,0:T(8,128)(2,1)}, u32[]{:S(2)}) copy-start(bf16[512,1024]{1,0:T(8,128)(2,1)} %param.26) | copy-start | bytes 3145732
Sparse Core Ops, SparseCore 0:
  52.0 22.6 all-reduce.7
  107.8 24.4 all-reduce.9
  136.2 63.2 reduce-scatter.17
  202.8 63.0 reduce-scatter.19
  269.3 67.3 reduce-scatter.13
  340.5 63.2 reduce-scatter.15
  406.4 27.2 all-reduce.11
  437.3 76.0 reduce-scatter.11
where the time goes:
time: 531 us; the launch traced here: 523 us
  waiting for transfers between devices  295 us (56%)
  matrix products  85 us (16%)
  other arithmetic  41.2 us (8%)
  local copies, waits for them, and re-layouts  35.9 us (7%)
  starting transfers between devices  28 us (5%)
  blocking collectives  22 us (4%)
  between operations  16 us (3%)
    unnamed x11, waiting for transfers between devices  113 us
    reduce_scatter x1, waiting for transfers between devices, local(): lax.psum_scatter(conv_in_local.astype(jnp.bfloat16), 'tm', scatter_dimens...  69 us
    psum x3, waiting for transfers between devices, model_sum(): return lax.psum(partial_sum, 'mp')  51.5 us
    reduce_scatter x1, waiting for transfers between devices, local(): lax.psum_scatter(qkv_local.astype(jnp.bfloat16), 'tm', scatter_dimension=...  48.6 us
    unnamed x84, local copies, waits for them, and re-layouts  27 us
    unnamed x1, blocking collectives  22 us
    ppermute x5, starting transfers between devices, extended(): before = lax.ppermute(last, axis, up)  20.6 us
    dot_general x1, matrix products, local(): jnp.einsum('hqk,khd->qhd', grad_scores, window[:, 0], preferred_element_t...  18.2 us
  transfers between devices with their start and end apart: 18, of which 11 were waited for; matrix products, arithmetic and copies ran while one was open for 22% of the time, Pallas kernels for 0%

commit v1 on v0

--- a/solution.py
+++ b/solution.py
@@ -62,7 +62,31 @@
 
 
 def model_sum(partial_sum):
-    return lax.psum(partial_sum, "mp")
+    size = lax.axis_size("mp")
+    if size != 2:
+        return lax.psum(partial_sum, "mp")
+    own = partial_sum.astype(jnp.bfloat16)
+    other = lax.ppermute(own, "mp", [(0, 1), (1, 0)])
+    return own.astype(jnp.float32) + other.astype(jnp.float32)
+
+
+def scatter_sum(parts, wire=jnp.bfloat16):
+    devices = lax.axis_size("tm")
+    rest = parts.shape[1:]
+    if devices & (devices - 1):
+        return lax.psum_scatter(parts.astype(wire), "tm", scatter_dimension=0).astype(jnp.float32)
+    place = lax.axis_index("tm")
+    left, bit = devices, 1
+    held = parts
+    while left > 1:
+        pairs = held.reshape((left // 2, 2) + rest)
+        mine = (place // bit) % 2
+        sent = lax.dynamic_index_in_dim(pairs, 1 - mine, 1, keepdims=False).astype(wire)
+        kept = lax.dynamic_index_in_dim(pairs, mine, 1, keepdims=False)
+        got = lax.ppermute(sent, "tm", [(i, i ^ bit) for i in range(devices)])
+        held = kept.astype(jnp.float32) + got.astype(jnp.float32)
+        left, bit = left // 2, bit * 2
+    return held[0]
 
 
 def conv_edges(signal):
@@ -214,29 +238,33 @@
         grad_norm_attn, gain_attn, normed_attn, inverse_attn
     )
     grad_frames = (grad_hidden + back_attn).astype(bf16)
-    grad_qkv, grad_proj, grad_gain_attn, grad_conv_in, grad_depth, grad_conv_out, grad_gain_conv = (
-        lax.psum_scatter(
-            qkv_local.astype(jnp.bfloat16), "tm", scatter_dimension=0, tiled=True
-        ).astype(jnp.float32),
-        lax.psum_scatter(
-            proj_local.astype(jnp.bfloat16), "tm", scatter_dimension=1, tiled=True
-        ).astype(jnp.float32),
-        lax.psum_scatter(
-            gain_attn_local.astype(jnp.bfloat16), "tm", scatter_dimension=0, tiled=True
-        ).astype(jnp.float32),
-        lax.psum_scatter(
-            conv_in_local.astype(jnp.bfloat16), "tm", scatter_dimension=0, tiled=True
-        ).astype(jnp.float32),
-        lax.psum_scatter(
-            depth_local.astype(jnp.bfloat16), "tm", scatter_dimension=1, tiled=True
-        ).astype(jnp.float32),
-        lax.psum_scatter(
-            conv_out_local.astype(jnp.bfloat16), "tm", scatter_dimension=1, tiled=True
-        ).astype(jnp.float32),
-        lax.psum_scatter(
-            gain_conv_local.astype(jnp.bfloat16), "tm", scatter_dimension=0, tiled=True
-        ).astype(jnp.float32),
-    )
+    devices = lax.axis_size("tm")
+
+    def by_rows(array):
+        return array.reshape((devices, array.shape[0] // devices) + array.shape[1:])
+
+    def by_columns(array):
+        rows, columns = array.shape
+        return array.reshape(rows, devices, columns // devices).transpose(1, 0, 2)
+
+    grad_qkv = scatter_sum(by_rows(qkv_local))
+    grad_proj = scatter_sum(by_columns(proj_local))
+    grad_conv_in = scatter_sum(by_rows(conv_in_local))
+    grad_conv_out = scatter_sum(by_columns(conv_out_local))
+    tap_part = local_width // devices
+    gain_part = model_width // devices
+    small = jnp.concatenate(
+        [
+            gain_attn_local.reshape(devices, gain_part),
+            gain_conv_local.reshape(devices, gain_part),
+            by_columns(depth_local).reshape(devices, KERNEL * tap_part),
+        ],
+        axis=1,
+    )
+    small = scatter_sum(small, f32)
+    grad_gain_attn = small[:gain_part]
+    grad_gain_conv = small[gain_part : 2 * gain_part]
+    grad_depth = small[2 * gain_part :].reshape(KERNEL, tap_part)
     return (
         output,
         grad_frames,

time: 531 us -> 314 us (0.59)
  waiting for transfers between devices: 295 us -> 85.9 us
  blocking collectives: 22 us -> 0 us
  starting transfers between devices: 28 us -> 49.6 us
  other arithmetic: 41.2 us -> 56.8 us
  between operations: 16 us -> 2.04 us
  matrix products: 85 us -> 71.7 us
  local copies, waits for them, and re-layouts: 35.9 us -> 43.8 us
    reduce_scatter x2 -> x0, waiting for transfers between devices: 118 us -> none  [the longest x1 69 us: local(): lax.psum_scatter(conv_in_local.astype(jnp.bfloat16), 'tm', scatter_dimens...]
    unnamed x11 -> x0, waiting for transfers between devices: 113 us -> none
    ppermute x0 -> x19, waiting for transfers between devices: none -> 72.7 us  [the longest x15 72.7 us: scatter_sum(): got = lax.ppermute(sent, 'tm', [(i, i ^ bit) for i in range(devices)])]
    psum x3 -> x0, waiting for transfers between devices: 51.5 us -> none  [model_sum(): return lax.psum(partial_sum, 'mp')]
    unnamed x1 -> x0, blocking collectives: 22 us -> none
    ppermute x0 -> x19, starting transfers between devices: none -> 21.3 us  [the longest x15 21.2 us: scatter_sum(): got = lax.ppermute(sent, 'tm', [(i, i ^ bit) for i in range(devices)])]
    add x1 -> x11, other arithmetic: 0.79 us -> 11.6 us  [scatter_sum(): held = kept.astype(jnp.float32) + got.astype(jnp.float32)]
    convert_element_type x7 -> x0, other arithmetic: 8.34 us -> none  [the longest x6 5.22 us: local(): grad_qkv, grad_proj, grad_gain_attn, grad_conv_in, grad_depth, grad_conv_...]
  transfers between devices with their start and end apart: 18 -> 29, of which waited for: 11 -> 9; matrix products, arithmetic and copies ran while one was open for 22% -> 41% of each run, Pallas kernels for 0% -> 0%
where the time goes in v1:
time: 314 us; the launch traced here: 310 us
  waiting for transfers between devices  85.9 us (27%)
  matrix products  71.7 us (23%)
  other arithmetic  56.8 us (18%)
  starting transfers between devices  49.6 us (16%)
  local copies, waits for them, and re-layouts  43.8 us (14%)
    ppermute x15, waiting for transfers between devices, scatter_sum(): got = lax.ppermute(sent, 'tm', [(i, i ^ bit) for i in range(devices)])  72.7 us
    ppermute x5, starting transfers between devices, extended(): before = lax.ppermute(last, axis, up)  21.6 us
    ppermute x15, starting transfers between devices, scatter_sum(): got = lax.ppermute(sent, 'tm', [(i, i ^ bit) for i in range(devices)])  21.2 us
    dot_general x1, matrix products, local(): jnp.einsum('hqk,khd->qhd', grad_scores, window[:, 0], preferred_element_t...  20.8 us
    unnamed x123, local copies, waits for them, and re-layouts  19.4 us
    dot_general x1, matrix products, local(): jnp.einsum('hqk,qhd->khd', grad_scores, query_rows, preferred_element_typ...  18.2 us
    add x11, other arithmetic, scatter_sum(): held = kept.astype(jnp.float32) + got.astype(jnp.float32)  11.6 us
    ppermute x5, waiting for transfers between devices, extended(): before = lax.ppermute(last, axis, up)  8.11 us
  transfers between devices with their start and end apart: 29, of which 9 were waited for; matrix products, arithmetic and copies ran while one was open for 41% of the time, Pallas kernels for 0%

profile of v1, /device:TPU:0, one launch (start us, length us, event | category | flops | bytes accessed | tf_op | source)
XLA Modules:
  0.0 309.8 jit_solution(12341376995531415573)
XLA Ops:
  1.4 4.9 %collective-permute-start.2 = (bf16[128]{0:T(256)(128)(2,1)S(1)}, bf16[128]{0:T(256)(128)(2,1)S(1)}, u32[]{:S(2)}, u32[]{:S(2)}) collective-permute-start(bf16[128]{0:T(256)(128)(2,1)S(1)} %get-tuple-element.106), channel_id=1, source_target_pairs={{0,2},{2,4},{4,6},{6,8},{8,10},{10,12},{12,14},{1,3},{3,5},{5,7},{... | collective-permute-start | bytes 776 | tf_op jit(solution)/shard_map/ppermute | solution.py:22
  9.1 1.6 fusion.29
  10.8 4.7 %copy.54 = bf16[1024,3,512]{0,2,1:T(8,128)(2,1)} copy(bf16[1024,3,512]{2,0,1:T(8,128)(2,1)} %param.20) | data formatting | bytes 6291456 | tf_op args[2]
  15.5 5.0 %convolution_convert_fusion = bf16[512,1536]{1,0:T(8,128)(2,1)} fusion(bf16[1024,1536]{0,1:T(8,128)(2,1)} %bitcast.219, bf16[512,1024]{1,0:T(8,128)(2,1)S(1)} %copy-done.2, f32[1024]{0:T(1024)S(1)} %copy-done.49, f32[512]{0:T(512)S(1)} %add_rsqrt_fusion.1, f32[512]{0:T(512)S(1)} %broadcast_multiply_fusion.5), kind=kOutput, calls=%fused_computation.36 | convolution fusion | flops 1614020608 | bytes 5775360 | tf_op jit(solution)/shard_map/dot_general | solution.py:116
  20.5 3.0 reshape.366
  23.7 4.6 %collective-permute-start = (bf16[128,2,4,128]{3,0,2,1:T(8,128)(2,1)S(1)}, bf16[128,2,4,128]{3,0,2,1:T(8,128)(2,1)S(1)}, u32[]{:S(2)}, u32[]{:S(2)}) collective-permute-start(bf16[128,2,4,128]{3,0,2,1:T(8,128)(2,1)S(1)} %copy.89), channel_id=1, source_target_pairs={{0,2},{2,4},{4,6},{6,8},{8,10},{10,12},{12,14},{1,3},{3,5},{5,7},{... | collective-permute-start | bytes 786440 | tf_op jit(solution)/shard_map/ppermute | solution.py:22
  28.3 1.5 collective-permute-start.1
  30.8 8.1 %collective-permute-done = bf16[128,2,4,128]{3,0,2,1:T(8,128)(2,1)S(1)} collective-permute-done((bf16[128,2,4,128]{3,0,2,1:T(8,128)(2,1)S(1)}, bf16[128,2,4,128]{3,0,2,1:T(8,128)(2,1)S(1)}, u32[]{:S(2)}, u32[]{:S(2)}) %collective-permute-start) | collective-permute-done | bytes 262176 | tf_op jit(solution)/shard_map/ppermute | solution.py:22
  40.2 2.9 fusion.137
  45.8 1.7 convolution_convert_fusion.3
  48.4 2.6 copy.60
  51.0 2.3 fusion.129
  58.8 4.3 %collective-permute-start.5 = (bf16[4,512]{1,0:T(4,128)(2,1)S(1)}, bf16[4,512]{1,0:T(4,128)(2,1)S(1)}, u32[]{:S(2)}, u32[]{:S(2)}) collective-permute-start(bf16[4,512]{1,0:T(4,128)(2,1)S(1)} %get-tuple-element.87), channel_id=1, source_target_pairs={{0,2},{2,4},{4,6},{6,8},{8,10},{10,12},{12,14},{1,3},{3,5},{5,7},{... | collective-permute-start | bytes 12296 | tf_op jit(solution)/shard_map/ppermute | solution.py:22
  64.6 5.1 %collective-permute-done.6 = bf16[4,512]{1,0:T(4,128)(2,1)S(1)} collective-permute-done((bf16[4,512]{1,0:T(4,128)(2,1)S(1)}, bf16[4,512]{1,0:T(4,128)(2,1)S(1)}, u32[]{:S(2)}, u32[]{:S(2)}) %collective-permute-start.6) | collective-permute-done | bytes 4128 | tf_op jit(solution)/shard_map/ppermute | solution.py:23
  69.7 4.2 %fusion.69 = f32[512,512]{1,0:T(8,128)S(1)} fusion(bf16[512,512]{1,0:T(8,128)(2,1)} %copy-done.26, bf16[4,512]{1,0:T(4,128)(2,1)S(1)} %collective-permute-done.6, bf16[4,512]{1,0:T(4,128)(2,1)S(1)} %collective-permute-done.5, f32[512]{0:T(512)S(1)} %bitcast.245, f32[512]{0:T(512)S(1)} %bitcast.247, f32[512]{0:T(512)S(1)} %bitcast.233, f32[512]{0:T(512)S(1)} %bitcast.235, ...), kind=kLoop, calls=%fused_computation.113 | loop fusion | flops 13107200 | bytes 1599488 | tf_op jit(solution)/shard_map/add | solution.py:148
  73.9 2.1 convolution_bitcast_fusion
  76.0 2.4 fusion.85
  79.8 5.6 %collective-permute-start.9 = (bf16[4,512]{1,0:T(4,128)(2,1)S(1)}, bf16[4,512]{1,0:T(4,128)(2,1)S(1)}, u32[]{:S(2)}, u32[]{:S(2)}) collective-permute-start(bf16[4,512]{1,0:T(4,128)(2,1)S(1)} %get-tuple-element.86), channel_id=1, source_target_pairs={{0,2},{2,4},{4,6},{6,8},{8,10},{10,12},{12,14},{1,3},{3,5},{5,7},{... | collective-permute-start | bytes 12296 | tf_op jit(solution)/shard_map/ppermute | solution.py:22
  85.6 3.0 collective-permute-start.26
  88.6 2.5 multiply_bitcast_fusion.1
  91.6 1.5 copy-done.29
  93.1 2.3 bitcast_convert_fusion
  95.4 3.6 %collective-permute-done.26 = bf16[4,512,128]{2,1,0:T(8,128)(2,1)S(1)} collective-permute-done((bf16[4,512,128]{2,1,0:T(8,128)(2,1)S(1)}, bf16[4,512,128]{2,1,0:T(8,128)(2,1)S(1)}, u32[]{:S(2)}, u32[]{:S(2)}) %collective-permute-start.26) | collective-permute-done | bytes 524320 | tf_op jit(solution)/shard_map/ppermute | solution.py:86
  99.9 1.6 collective-permute-start.27
  101.5 1.7 convolution_convert_fusion.2
  108.6 1.8 collective-permute-start.28
  110.3 4.0 %multiply_reduce_fusion.1 = (f32[1024]{0:T(1024)}, f32[512]{0:T(512)S(1)}, f32[512]{0:T(512)S(1)}, bf16[1024,512]{0,1:T(8,128)(2,1)}) fusion(bf16[512,1024]{1,0:T(8,128)(2,1)} %collective-permute-done.10, bf16[512,1024]{1,0:T(8,128)(2,1)} %bitcast_convert_fusion, f32[512,1024]{1,0:T(8,128)S(1)} %get-tuple-element.77, f32[512]{0:T(512)S(1)} %add_rsqrt_fusion, ...), kind=kLoop, calls=%fused_computation.59 | loop fusion | flops 6813696 | bytes 5259264 | tf_op jit(solution)/shard_map/reduce_sum | solution.py:42
  114.4 3.8 %convert_bitcast_fusion = (bf16[1024,512]{0,1:T(8,128)(2,1)}, f32[512,1024]{1,0:T(8,128)S(1)}, bf16[512,1024]{1,0:T(8,128)(2,1)}) fusion(f32[512]{0:T(512)S(1)} %get-tuple-element.111, f32[512,1024]{1,0:T(8,128)S(1)} %get-tuple-element.77, f32[512]{0:T(512)S(1)} %broadcast_multiply_fusion.4, f32[512]{0:T(512)S(1)} %get-tuple-element.112, ...), kind=kLoop, calls=%fused_computation.204 | loop fusion | flops 9437184 | bytes 11546624 | tf_op jit(solution)/shard_map/dot_general | solution.py:194
  121.7 3.7 %fusion.95 = f32[4,512,768]{2,1,0:T(8,128)} fusion(bf16[512,4,128]{0,2,1:T(8,128)(2,1)S(1)} %bitcast.224, bf16[768,2,4,128]{3,0,2,1:T(8,128)(2,1)S(1)} %copy-done.25), kind=kOutput, calls=%fused_computation.169 | convolution fusion | flops 402653184 | bytes 7602176 | tf_op jit(solution)/shard_map/qhd,khd->hqk/dot_general | solution.py:203
  125.4 18.2 %fusion.50 = f32[768,1,4,128]{0,3,2,1:T(8,128)} fusion(f32[4,512,768]{2,1,0:T(8,128)} %fusion.95, bf16[512,1,4,128]{3,2,1,0:T(4,128)(2,1)S(1)} %copy-done.34, f32[4,512,768]{2,1,0:T(8,128)} %copy-done.52, f32[4,512]{1,0:T(4,128)S(1)} %copy-done.54), kind=kOutput, calls=%fused_computation.86 | convolution fusion | flops 413666048 | bytes 14688256 | tf_op jit(solution)/shard_map/hqk,qhd->khd/dot_general | solution.py:209
  143.6 2.9 fusion.6
  146.5 1.7 fusion.30
  148.2 1.6 copy.83
  152.7 1.7 collective-permute-start.17
  154.4 2.7 copy.84
  158.2 2.3 collective-permute-start.11
  161.7 2.5 fusion.90
  164.2 1.9 copy-done.11
  167.3 3.1 collective-permute-start.23
  170.3 20.8 %fusion.53 = bf16[512,1,4,128]{0,3,2,1:T(8,128)(2,1)S(1)} fusion(f32[4,512,768]{2,1,0:T(8,128)} %fusion.95, bf16[768,2,4,128]{3,0,2,1:T(8,128)(2,1)} %copy-done.24, f32[4,512,768]{2,1,0:T(8,128)} %copy-done.52, f32[4,512]{1,0:T(4,128)} %copy-done.53), kind=kOutput, calls=%fused_computation.90 | convolution fusion | flops 413666048 | bytes 26492928 | tf_op jit(solution)/shard_map/hqk,khd->qhd/dot_general | solution.py:208
  191.1 1.8 fusion.113
  193.0 2.0 fusion.114
  195.0 1.9 maximum_convert_fusion
  197.2 1.9 bitcast_add_fusion.5
  199.2 1.5 collective-permute-start.18
  200.7 1.8 convolution_convert_fusion.1
  202.6 4.2 %collective-permute-done.18 = bf16[2,512,128]{2,1,0:T(8,128)(2,1)S(1)} collective-permute-done((bf16[2,512,128]{2,1,0:T(8,128)(2,1)S(1)}, bf16[2,512,128]{2,1,0:T(8,128)(2,1)S(1)}, u32[]{:S(2)}, u32[]{:S(2)}) %collective-permute-start.18) | collective-permute-done | bytes 262176 | tf_op jit(solution)/shard_map/ppermute | solution.py:86
  208.3 1.6 add_bitcast_fusion.2
  209.9 4.7 %collective-permute-done.19 = bf16[1,512,128]{2,1,0:T(8,128)(2,1)S(1)} collective-permute-done((bf16[1,512,128]{2,1,0:T(8,128)(2,1)S(1)}, bf16[1,512,128]{2,1,0:T(8,128)(2,1)S(1)}, u32[]{:S(2)}, u32[]{:S(2)}) %collective-permute-start.19) | collective-permute-done | bytes 131104 | tf_op jit(solution)/shard_map/ppermute | solution.py:86
  215.3 1.6 bitcast_add_fusion.1
  217.0 2.1 fusion.28
  219.2 2.4 copy.82
  221.6 3.6 %fusion.138 = f32[4,2,128,3,512]{4,2,3,1,0:T(8,128)S(1)} fusion(bf16[4,2,128,512,1]{3,2,4,1,0:T(8,128)(2,1)} %bitcast.227, bf16[3,512,512,1,1]{2,1,0,4,3:T(8,128)(2,1)} %bitcast.226), kind=kOutput, calls=%fused_computation.260 | convolution fusion | flops 1610612736 | bytes 8912896 | tf_op jit(solution)/shard_map/dot_general | solution.py:231
  225.2 1.6 fusion.37
  231.4 29.9 %collective-permute-done.20 = f32[4,832]{1,0:T(4,128)S(1)} collective-permute-done((f32[4,832]{1,0:T(4,128)S(1)}, f32[4,832]{1,0:T(4,128)S(1)}, u32[]{:S(2)}, u32[]{:S(2)}) %collective-permute-start.20) | collective-permute-done | bytes 13344 | tf_op jit(solution)/shard_map/ppermute | solution.py:86
  261.5 3.6 %collective-permute-done.21 = f32[2,832]{1,0:T(2,128)S(1)} collective-permute-done((f32[2,832]{1,0:T(2,128)S(1)}, f32[2,832]{1,0:T(2,128)S(1)}, u32[]{:S(2)}, u32[]{:S(2)}) %collective-permute-start.21) | collective-permute-done | bytes 6688 | tf_op jit(solution)/shard_map/ppermute | solution.py:86
  265.2 3.1 bitcast_add_fusion
  268.4 1.6 collective-permute-start.15
  270.3 1.9 fusion.27
  272.9 2.3 bitcast_add_fusion.4
  275.4 3.0 collective-permute-start.25
  278.4 11.5 %collective-permute-done.15 = bf16[2,128,3,512]{3,1,2,0:T(8,128)(2,1)} collective-permute-done((bf16[2,128,3,512]{3,1,2,0:T(8,128)(2,1)S(1)}, bf16[2,128,3,512]{3,1,2,0:T(8,128)(2,1)}, u32[]{:S(2)}, u32[]{:S(2)}) %collective-permute-start.15) | collective-permute-done | bytes 786464 | tf_op jit(solution)/shard_map/ppermute | solution.py:86
  289.9 1.5 bitcast_add_fusion.2
  293.4 15.2 %collective-permute-done.16 = bf16[1,128,3,512]{3,1,2,0:T(8,128)(2,1)S(1)} collective-permute-done((bf16[1,128,3,512]{3,1,2,0:T(8,128)(2,1)S(1)}, bf16[1,128,3,512]{3,1,2,0:T(8,128)(2,1)S(1)}, u32[]{:S(2)}, u32[]{:S(2)}) %collective-permute-start.16) | collective-permute-done | bytes 393248 | tf_op jit(solution)/shard_map/ppermute | solution.py:86
  (228 shorter events, 46.1 us)
Async XLA Ops:
  0.6 75.4 %copy-start = (bf16[512,1024]{1,0:T(8,128)(2,1)S(1)}, bf16[512,1024]{1,0:T(8,128)(2,1)}, u32[]{:S(2)}) copy-start(bf16[512,1024]{1,0:T(8,128)(2,1)} %param.26) | copy-start | bytes 3145732
  1.4 28.9 %collective-permute-start.2 = (bf16[128]{0:T(256)(128)(2,1)S(1)}, bf16[128]{0:T(256)(128)(2,1)S(1)}, u32[]{:S(2)}, u32[]{:S(2)}) collective-permute-start(bf16[128]{0:T(256)(128)(2,1)S(1)} %get-tuple-element.106), channel_id=1, source_target_pairs={{0,2},{2,4},{4,6},{6,8},{8,10},{10,12},{12,14},{1,3},{3,5},{5,7},{... | collective-permute-start | bytes 776 | tf_op jit(solution)/shard_map/ppermute | solution.py:22
  6.3 24.1 %collective-permute-start.3 = (bf16[128]{0:T(256)(128)(2,1)S(1)}, bf16[128]{0:T(256)(128)(2,1)S(1)}, u32[]{:S(2)}, u32[]{:S(2)}) collective-permute-start(bf16[128]{0:T(256)(128)(2,1)S(1)} %get-tuple-element.107), channel_id=1, source_target_pairs={{2,0},{4,2},{6,4},{8,6},{10,8},{12,10},{14,12},{3,1},{5,3},{7,5},{... | collective-permute-start | bytes 776 | tf_op jit(solution)/shard_map/ppermute | solution.py:23
  10.7 4.8 %copy-start.2 = (bf16[512,1024]{1,0:T(8,128)(2,1)S(1)}, bf16[512,1024]{1,0:T(8,128)(2,1)}, u32[]{:S(2)}) copy-start(bf16[512,1024]{1,0:T(8,128)(2,1)} %param.18) | copy-start | bytes 3145732
  10.7 4.8 %copy-start.49 = (f32[1024]{0:T(1024)S(1)}, f32[1024]{0:T(1024)}, u32[]{:S(2)}) copy-start(f32[1024]{0:T(1024)} %param.22) | copy-start | bytes 12292
  23.7 15.2 %collective-permute-start = (bf16[128,2,4,128]{3,0,2,1:T(8,128)(2,1)S(1)}, bf16[128,2,4,128]{3,0,2,1:T(8,128)(2,1)S(1)}, u32[]{:S(2)}, u32[]{:S(2)}) collective-permute-start(bf16[128,2,4,128]{3,0,2,1:T(8,128)(2,1)S(1)} %copy.89), channel_id=1, source_target_pairs={{0,2},{2,4},{4,6},{6,8},{8,10},{10,12},{12,14},{1,3},{3,5},{5,7},{... | collective-permute-start | bytes 786440 | tf_op jit(solution)/shard_map/ppermute | solution.py:22
  28.3 10.8 %collective-permute-start.1 = (bf16[128,2,4,128]{3,0,2,1:T(8,128)(2,1)S(1)}, bf16[128,2,4,128]{3,0,2,1:T(8,128)(2,1)S(1)}, u32[]{:S(2)}, u32[]{:S(2)}) collective-permute-start(bf16[128,2,4,128]{3,0,2,1:T(8,128)(2,1)S(1)} %copy.91), channel_id=1, source_target_pairs={{2,0},{4,2},{6,4},{8,6},{10,8},{12,10},{14,12},{3,1},{5,3},{7,5},{... | collective-permute-start | bytes 786440 | tf_op jit(solution)/shard_map/ppermute | solution.py:23
  30.0 9.2 %copy-start.33 = (bf16[512,1,4,128]{3,2,1,0:T(4,128)(2,1)}, bf16[512,1,4,128]{3,2,1,0:T(4,128)(2,1)S(1)}, u32[]{:S(2)}) copy-start(bf16[512,1,4,128]{3,2,1,0:T(4,128)(2,1)S(1)} %slice.329) | copy-start | bytes 1572868
  39.2 3.9 %copy-start.24 = (bf16[768,2,4,128]{3,0,2,1:T(8,128)(2,1)}, bf16[768,2,4,128]{3,0,2,1:T(8,128)(2,1)S(1)}, u32[]{:S(2)}) copy-start(bf16[768,2,4,128]{3,0,2,1:T(8,128)(2,1)S(1)} %constant_dynamic-update-slice_fusion) | copy-start | bytes 4718596
  43.2 2.6 copy-start.52
  43.2 2.7 copy-start.53
  43.2 2.6 copy-start.40
  47.5 3.5 %collective-permute-start.4 = (bf16[512,1024]{1,0:T(8,128)(2,1)}, bf16[512,1024]{1,0:T(8,128)(2,1)}, u32[]{:S(2)}, u32[]{:S(2)}) collective-permute-start(bf16[512,1024]{1,0:T(8,128)(2,1)} %convolution_convert_fusion.3), channel_id=1, source_target_pairs={{0,1},{1,0},{2,3},{3,2},{4,5},{5,4},{6,7},{7,6},{8,9},{9,8},{10,11... | collective-permute-start | bytes 3145736 | tf_op jit(solution)/shard_map/ppermute | solution.py:69
  48.4 2.6 copy-start.51
  58.8 5.7 %collective-permute-start.5 = (bf16[4,512]{1,0:T(4,128)(2,1)S(1)}, bf16[4,512]{1,0:T(4,128)(2,1)S(1)}, u32[]{:S(2)}, u32[]{:S(2)}) collective-permute-start(bf16[4,512]{1,0:T(4,128)(2,1)S(1)} %get-tuple-element.87), channel_id=1, source_target_pairs={{0,2},{2,4},{4,6},{6,8},{8,10},{10,12},{12,14},{1,3},{3,5},{5,7},{... | collective-permute-start | bytes 12296 | tf_op jit(solution)/shard_map/ppermute | solution.py:22
  63.2 6.5 %collective-permute-start.6 = (bf16[4,512]{1,0:T(4,128)(2,1)S(1)}, bf16[4,512]{1,0:T(4,128)(2,1)S(1)}, u32[]{:S(2)}, u32[]{:S(2)}) collective-permute-start(bf16[4,512]{1,0:T(4,128)(2,1)S(1)} %get-tuple-element.88), channel_id=1, source_target_pairs={{2,0},{4,2},{6,4},{8,6},{10,8},{12,10},{14,12},{3,1},{5,3},{7,5},{... | collective-permute-start | bytes 12296 | tf_op jit(solution)/shard_map/ppermute | solution.py:23
  78.5 10.1 %collective-permute-start.8 = (bf16[4,512]{1,0:T(4,128)(2,1)S(1)}, bf16[4,512]{1,0:T(4,128)(2,1)S(1)}, u32[]{:S(2)}, u32[]{:S(2)}) collective-permute-start(bf16[4,512]{1,0:T(4,128)(2,1)S(1)} %get-tuple-element.85), channel_id=1, source_target_pairs={{2,0},{4,2},{6,4},{8,6},{10,8},{12,10},{14,12},{3,1},{5,3},{7,5},{... | collective-permute-start | bytes 12296 | tf_op jit(solution)/shard_map/ppermute | solution.py:23
  79.8 8.8 %copy-start.8 = (f32[512,2,512]{2,0,1:T(8,128)S(1)}, f32[512,2,512]{2,0,1:T(8,128)}, u32[]{:S(2)}) copy-start(f32[512,2,512]{2,0,1:T(8,128)} %copy-done.7) | copy-start | bytes 6291460
  79.8 8.8 %collective-permute-start.9 = (bf16[4,512]{1,0:T(4,128)(2,1)S(1)}, bf16[4,512]{1,0:T(4,128)(2,1)S(1)}, u32[]{:S(2)}, u32[]{:S(2)}) collective-permute-start(bf16[4,512]{1,0:T(4,128)(2,1)S(1)} %get-tuple-element.86), channel_id=1, source_target_pairs={{0,2},{2,4},{4,6},{6,8},{8,10},{10,12},{12,14},{1,3},{3,5},{5,7},{... | collective-permute-start | bytes 12296 | tf_op jit(solution)/shard_map/ppermute | solution.py:22
  85.6 13.3 %collective-permute-start.26 = (bf16[4,512,128]{2,1,0:T(8,128)(2,1)S(1)}, bf16[4,512,128]{2,1,0:T(8,128)(2,1)S(1)}, u32[]{:S(2)}, u32[]{:S(2)}) collective-permute-start(bf16[4,512,128]{2,1,0:T(8,128)(2,1)S(1)} %fusion.109), channel_id=1, source_target_pairs={{0,2},{2,0},{4,6},{6,4},{8,10},{10,8},{12,14},{14,12},{1,3},{3,1},... | collective-permute-start | bytes 1572872 | tf_op jit(solution)/shard_map/ppermute | solution.py:86
  91.2 4.2 %copy-start.31 = (bf16[512,1,512]{2,0,1:T(8,128)(2,1)}, bf16[512,1,512]{2,0,1:T(8,128)(2,1)S(1)}, u32[]{:S(2)}) copy-start(bf16[512,1,512]{2,0,1:T(8,128)(2,1)S(1)} %get-tuple-element.74) | copy-start | bytes 1572868
  91.6 3.8 %copy-start.32 = (bf16[512,1,512]{2,0,1:T(8,128)(2,1)}, bf16[512,1,512]{2,0,1:T(8,128)(2,1)S(1)}, u32[]{:S(2)}) copy-start(bf16[512,1,512]{2,0,1:T(8,128)(2,1)S(1)} %multiply_bitcast_fusion) | copy-start | bytes 1572868
  95.4 14.9 %collective-permute-start.10 = (bf16[512,1024]{1,0:T(8,128)(2,1)}, bf16[512,1024]{1,0:T(8,128)(2,1)}, u32[]{:S(2)}, u32[]{:S(2)}) collective-permute-start(bf16[512,1024]{1,0:T(8,128)(2,1)} %bitcast_convert_fusion), channel_id=1, source_target_pairs={{0,1},{1,0},{2,3},{3,2},{4,5},{5,4},{6,7},{7,6},{8,9},{9,8},{10,11... | collective-permute-start | bytes 3145736 | tf_op jit(solution)/shard_map/ppermute | solution.py:69
  99.1 4.2 %copy-start.22 = (f32[4,512,128]{2,1,0:T(8,128)}, f32[4,512,128]{2,1,0:T(8,128)S(1)}, u32[]{:S(2)}) copy-start(f32[4,512,128]{2,1,0:T(8,128)S(1)} %bitcast_add_fusion.3) | copy-start | bytes 3145732
  99.9 7.5 %collective-permute-start.27 = (bf16[2,512,128]{2,1,0:T(8,128)(2,1)}, bf16[2,512,128]{2,1,0:T(8,128)(2,1)S(1)}, u32[]{:S(2)}, u32[]{:S(2)}) collective-permute-start(bf16[2,512,128]{2,1,0:T(8,128)(2,1)} %fusion.117), channel_id=1, source_target_pairs={{0,4},{2,6},{4,0},{6,2},{8,12},{10,14},{12,8},{14,10},{1,5},{3,7},... | collective-permute-start | bytes 786440 | tf_op jit(solution)/shard_map/ppermute | solution.py:86
  104.7 9.7 %collective-permute-start.7 = (bf16[512,1024]{1,0:T(8,128)(2,1)}, bf16[512,1024]{1,0:T(8,128)(2,1)}, u32[]{:S(2)}, u32[]{:S(2)}) collective-permute-start(bf16[512,1024]{1,0:T(8,128)(2,1)} %convolution_convert_fusion.2), channel_id=1, source_target_pairs={{0,1},{1,0},{2,3},{3,2},{4,5},{5,4},{6,7},{7,6},{8,9},{9,8},{10,11... | collective-permute-start | bytes 3145736 | tf_op jit(solution)/shard_map/ppermute | solution.py:69
  108.5 5.9 %copy-start.35 = (f32[2,512,128]{2,1,0:T(8,128)}, f32[2,512,128]{2,1,0:T(8,128)S(1)}, u32[]{:S(2)}) copy-start(f32[2,512,128]{2,1,0:T(8,128)S(1)} %bitcast_add_fusion.6) | copy-start | bytes 1572868
  108.5 5.9 %copy-start.39 = (bf16[512,1024]{1,0:T(8,128)(2,1)S(1)}, bf16[512,1024]{1,0:T(8,128)(2,1)}, u32[]{:S(2)}) copy-start(bf16[512,1024]{1,0:T(8,128)(2,1)} %param.27) | copy-start | bytes 3145732
  108.5 5.9 %copy-start.42 = (bf16[512,1024]{1,0:T(8,128)(2,1)S(1)}, bf16[512,1024]{1,0:T(8,128)(2,1)}, u32[]{:S(2)}) copy-start(bf16[512,1024]{1,0:T(8,128)(2,1)} %convolution_convert_fusion.2) | copy-start | bytes 3145732
  108.5 5.9 %copy-start.47 = (f32[1024]{0:T(1024)S(1)}, f32[1024]{0:T(1024)}, u32[]{:S(2)}) copy-start(f32[1024]{0:T(1024)} %param.25) | copy-start | bytes 12292
  108.6 99.8 %collective-permute-start.28 = (bf16[1,512,128]{2,1,0:T(8,128)(2,1)S(1)}, bf16[1,512,128]{2,1,0:T(8,128)(2,1)}, u32[]{:S(2)}, u32[]{:S(2)}) collective-permute-start(bf16[1,512,128]{2,1,0:T(8,128)(2,1)S(1)} %dynamic-slice_convert_fusion.8), channel_id=1, source_target_pairs={{0,8},{2,10},{4,12},{6,14},{8,0},{10,2},{12,4},{14,6},{1,9},{3,11}... | collective-permute-start | bytes 393224 | tf_op jit(solution)/shard_map/ppermute | solution.py:86
  110.3 10.0 %slice-start = ((s8[6291456]{0:T(1024)(128)(4,1)}), s8[4194304]{0:T(1024)(128)(4,1)S(1)}, s32[]{:S(2)}) async-start(s8[6291456]{0:T(1024)(128)(4,1)} %bitcast.253), calls=%async_computation | async-start | bytes 8388608
  114.4 5.1 %copy-start.41 = (bf16[512,1024]{1,0:T(8,128)(2,1)S(1)}, bf16[512,1024]{1,0:T(8,128)(2,1)}, u32[]{:S(2)}) copy-start(bf16[512,1024]{1,0:T(8,128)(2,1)} %param.21) | copy-start | bytes 3145732
  114.4 5.9 %slice-start.1 = ((s8[6291456]{0:T(1024)(128)(4,1)}), s8[2097152]{0:T(1024)(128)(4,1)S(1)}, s32[]{:S(2)}) async-start(s8[6291456]{0:T(1024)(128)(4,1)} %bitcast.253), calls=%async_computation.1 | async-start | bytes 4194304
  121.7 3.7 %copy-start.34 = (bf16[512,1,4,128]{3,2,1,0:T(4,128)(2,1)S(1)}, bf16[512,1,4,128]{3,2,1,0:T(4,128)(2,1)}, u32[]{:S(2)}) copy-start(bf16[512,1,4,128]{3,2,1,0:T(4,128)(2,1)} %copy-done.33) | copy-start | bytes 1572868
  143.6 2.9 copy-start.6
  151.9 9.9 %copy-start.16 = (bf16[512,2,512]{0,2,1:T(8,128)(2,1)S(1)}, bf16[512,2,512]{0,2,1:T(8,128)(2,1)}, u32[]{:S(2)}) copy-start(bf16[512,2,512]{0,2,1:T(8,128)(2,1)} %copy.69) | copy-start | bytes 3145732
  152.7 44.2 %collective-permute-start.17 = (bf16[4,512,128]{2,1,0:T(8,128)(2,1)}, bf16[4,512,128]{2,1,0:T(8,128)(2,1)}, u32[]{:S(2)}, u32[]{:S(2)}) collective-permute-start(bf16[4,512,128]{2,1,0:T(8,128)(2,1)} %fusion.110), channel_id=1, source_target_pairs={{0,2},{2,0},{4,6},{6,4},{8,10},{10,8},{12,14},{14,12},{1,3},{3,1},... | collective-permute-start | bytes 1572872 | tf_op jit(solution)/shard_map/ppermute | solution.py:86
  158.2 33.0 %collective-permute-start.11 = (bf16[128,2,4,128]{0,3,2,1:T(8,128)(2,1)S(1)}, bf16[128,2,4,128]{0,3,2,1:T(8,128)(2,1)S(1)}, u32[]{:S(2)}, u32[]{:S(2)}) collective-permute-start(bf16[128,2,4,128]{0,3,2,1:T(8,128)(2,1)S(1)} %get-tuple-element.80), channel_id=1, source_target_pairs={{0,2},{2,4},{4,6},{6,8},{8,10},{10,12},{12,14},{1,3},{3,5},{5,7},{... | collective-permute-start | bytes 786440 | tf_op jit(solution)/shard_map/ppermute | solution.py:22
  160.4 30.7 %collective-permute-start.12 = (bf16[128,2,4,128]{0,3,2,1:T(8,128)(2,1)S(1)}, bf16[128,2,4,128]{0,3,2,1:T(8,128)(2,1)}, u32[]{:S(2)}, u32[]{:S(2)}) collective-permute-start(bf16[128,2,4,128]{0,3,2,1:T(8,128)(2,1)S(1)} %get-tuple-element.81), channel_id=1, source_target_pairs={{2,0},{4,2},{6,4},{8,6},{10,8},{12,10},{14,12},{3,1},{5,3},{7,5},{... | collective-permute-start | bytes 786440 | tf_op jit(solution)/shard_map/ppermute | solution.py:23
  167.3 48.1 %collective-permute-start.23 = (bf16[4,128,2,512]{3,1,2,0:T(8,128)(2,1)}, bf16[4,128,2,512]{3,1,2,0:T(8,128)(2,1)}, u32[]{:S(2)}, u32[]{:S(2)}) collective-permute-start(bf16[4,128,2,512]{3,1,2,0:T(8,128)(2,1)} %fusion.70), channel_id=1, source_target_pairs={{0,2},{2,0},{4,6},{6,4},{8,10},{10,8},{12,14},{14,12},{1,3},{3,1},... | collective-permute-start | bytes 3145736 | tf_op jit(solution)/shard_map/ppermute | solution.py:86
  196.9 5.6 %copy-start.37 = (bf16[512,3,4,128]{0,3,2,1:T(8,128)(2,1)}, bf16[512,3,4,128]{0,3,2,1:T(8,128)(2,1)S(1)}, u32[]{:S(2)}) copy-start(bf16[512,3,4,128]{0,3,2,1:T(8,128)(2,1)S(1)} %maximum_convert_fusion) | copy-start | bytes 4718596
  196.9 3.7 %copy-start.23 = (bf16[1024,3,512]{0,2,1:T(8,128)(2,1)S(1)}, bf16[1024,3,512]{0,2,1:T(8,128)(2,1)}, u32[]{:S(2)}) copy-start(bf16[1024,3,512]{0,2,1:T(8,128)(2,1)} %copy.54) | copy-start | bytes 9437188
  199.2 7.7 %collective-permute-start.18 = (bf16[2,512,128]{2,1,0:T(8,128)(2,1)S(1)}, bf16[2,512,128]{2,1,0:T(8,128)(2,1)S(1)}, u32[]{:S(2)}, u32[]{:S(2)}) collective-permute-start(bf16[2,512,128]{2,1,0:T(8,128)(2,1)S(1)} %fusion.116), channel_id=1, source_target_pairs={{0,4},{2,6},{4,0},{6,2},{8,12},{10,14},{12,8},{14,10},{1,5},{3,7},... | collective-permute-start | bytes 786440 | tf_op jit(solution)/shard_map/ppermute | solution.py:86
  200.7 7.6 %copy-start.36 = (f32[2,512,128]{2,1,0:T(8,128)S(1)}, f32[2,512,128]{2,1,0:T(8,128)}, u32[]{:S(2)}) copy-start(f32[2,512,128]{2,1,0:T(8,128)} %copy-done.35) | copy-start | bytes 1572868
  200.7 14.7 %copy-start.12 = (f32[4,2,128,2,512]{4,2,3,1,0:T(8,128)S(1)}, f32[4,2,128,2,512]{4,2,3,1,0:T(8,128)}, u32[]{:S(2)}) copy-start(f32[4,2,128,2,512]{4,2,3,1,0:T(8,128)} %copy-done.11) | copy-start | bytes 12582916
  202.5 14.5 %copy-start.17 = (bf16[512,1024]{1,0:T(8,128)(2,1)}, bf16[512,1024]{1,0:T(8,128)(2,1)S(1)}, u32[]{:S(2)}) copy-start(bf16[512,1024]{1,0:T(8,128)(2,1)S(1)} %convolution_convert_fusion.1) | copy-start | bytes 3145732
  202.5 14.5 %collective-permute-start.13 = (bf16[512,1024]{1,0:T(8,128)(2,1)S(1)}, bf16[512,1024]{1,0:T(8,128)(2,1)S(1)}, u32[]{:S(2)}, u32[]{:S(2)}) collective-permute-start(bf16[512,1024]{1,0:T(8,128)(2,1)S(1)} %convolution_convert_fusion.1), channel_id=1, source_target_pairs={{0,1},{1,0},{2,3},{3,2},{4,5},{5,4},{6,7},{7,6},{8,9},{9,8},{10,11... | collective-permute-start | bytes 3145736 | tf_op jit(solution)/shard_map/ppermute | solution.py:69
  206.9 7.7 %collective-permute-start.19 = (bf16[1,512,128]{2,1,0:T(8,128)(2,1)S(1)}, bf16[1,512,128]{2,1,0:T(8,128)(2,1)S(1)}, u32[]{:S(2)}, u32[]{:S(2)}) collective-permute-start(bf16[1,512,128]{2,1,0:T(8,128)(2,1)S(1)} %dynamic-slice_convert_fusion.9), channel_id=1, source_target_pairs={{0,8},{2,10},{4,12},{6,14},{8,0},{10,2},{12,4},{14,6},{1,9},{3,11}... | collective-permute-start | bytes 393224 | tf_op jit(solution)/shard_map/ppermute | solution.py:86
  225.2 5.6 %copy-start.21 = (f32[4,2,128,3,512]{4,2,3,1,0:T(8,128)}, f32[4,2,128,3,512]{4,2,3,1,0:T(8,128)S(1)}, u32[]{:S(2)}) copy-start(f32[4,2,128,3,512]{4,2,3,1,0:T(8,128)S(1)} %fusion.138) | copy-start | bytes 18874372
  226.8 38.4 %collective-permute-start.14 = (bf16[4,128,3,512]{3,1,2,0:T(8,128)(2,1)}, bf16[4,128,3,512]{3,1,2,0:T(8,128)(2,1)}, u32[]{:S(2)}, u32[]{:S(2)}) collective-permute-start(bf16[4,128,3,512]{3,1,2,0:T(8,128)(2,1)} %fusion.37), channel_id=1, source_target_pairs={{0,2},{2,0},{4,6},{6,4},{8,10},{10,8},{12,14},{14,12},{1,3},{3,1},... | collective-permute-start | bytes 4718600 | tf_op jit(solution)/shard_map/ppermute | solution.py:86
  229.7 43.3 %collective-permute-start.24 = (bf16[2,128,2,512]{3,2,1,0:T(2,128)(2,1)}, bf16[2,128,2,512]{3,2,1,0:T(2,128)(2,1)}, u32[]{:S(2)}, u32[]{:S(2)}) collective-permute-start(bf16[2,128,2,512]{3,2,1,0:T(2,128)(2,1)} %bitcast.201), channel_id=1, source_target_pairs={{0,4},{2,6},{4,0},{6,2},{8,12},{10,14},{12,8},{14,10},{1,5},{3,7},... | collective-permute-start | bytes 1572872 | tf_op jit(solution)/shard_map/ppermute | solution.py:86
  230.9 30.4 %collective-permute-start.20 = (f32[4,832]{1,0:T(4,128)S(1)}, f32[4,832]{1,0:T(4,128)S(1)}, u32[]{:S(2)}, u32[]{:S(2)}) collective-permute-start(f32[4,832]{1,0:T(4,128)S(1)} %bitcast.251), channel_id=1, source_target_pairs={{0,2},{2,0},{4,6},{6,4},{8,10},{10,8},{12,14},{14,12},{1,3},{3,1},... | collective-permute-start | bytes 39944 | tf_op jit(solution)/shard_map/ppermute | solution.py:86
  261.4 3.7 %collective-permute-start.21 = (f32[2,832]{1,0:T(2,128)S(1)}, f32[2,832]{1,0:T(2,128)S(1)}, u32[]{:S(2)}, u32[]{:S(2)}) collective-permute-start(f32[2,832]{1,0:T(2,128)S(1)} %bitcast.252), channel_id=1, source_target_pairs={{0,4},{2,6},{4,0},{6,2},{8,12},{10,14},{12,8},{14,10},{1,5},{3,7},... | collective-permute-start | bytes 19976 | tf_op jit(solution)/shard_map/ppermute | solution.py:86
  265.1 7.1 %collective-permute-start.22 = (f32[1,832]{1,0:T(1,128)S(1)}, f32[1,832]{1,0:T(1,128)S(1)}, u32[]{:S(2)}, u32[]{:S(2)}) collective-permute-start(f32[1,832]{1,0:T(1,128)S(1)} %constant_dynamic-slice_fusion.1), channel_id=1, source_target_pairs={{0,8},{2,10},{4,12},{6,14},{8,0},{10,2},{12,4},{14,6},{1,9},{3,11}... | collective-permute-start | bytes 9992 | tf_op jit(solution)/shard_map/ppermute | solution.py:86
  265.2 4.9 %copy-start.5 = (f32[512,1024]{1,0:T(8,128)S(1)}, f32[512,1024]{1,0:T(8,128)}, u32[]{:S(2)}) copy-start(f32[512,1024]{1,0:T(8,128)} %copy-done.4) | copy-start | bytes 6291460
  265.2 4.9 %copy-start.20 = (bf16[512,1024]{1,0:T(8,128)(2,1)S(1)}, bf16[512,1024]{1,0:T(8,128)(2,1)}, u32[]{:S(2)}) copy-start(bf16[512,1024]{1,0:T(8,128)(2,1)} %copy-done.19) | copy-start | bytes 3145732
  268.3 3.9 %copy-start.13 = (f32[4,128,3,512]{3,1,2,0:T(8,128)}, f32[4,128,3,512]{3,1,2,0:T(8,128)S(1)}, u32[]{:S(2)}) copy-start(f32[4,128,3,512]{3,1,2,0:T(8,128)S(1)} %bitcast_add_fusion) | copy-start | bytes 9437188
  268.4 4.5 %copy-start.15 = (f32[2,1,128,2,512]{4,2,3,1,0:T(8,128)S(1)}, f32[2,1,128,2,512]{4,2,3,1,0:T(8,128)}, u32[]{:S(2)}) copy-start(f32[2,1,128,2,512]{4,2,3,1,0:T(8,128)} %constant_dynamic-slice_fusion) | copy-start | bytes 3145732
  268.4 21.4 %collective-permute-start.15 = (bf16[2,128,3,512]{3,1,2,0:T(8,128)(2,1)S(1)}, bf16[2,128,3,512]{3,1,2,0:T(8,128)(2,1)}, u32[]{:S(2)}, u32[]{:S(2)}) collective-permute-start(bf16[2,128,3,512]{3,1,2,0:T(8,128)(2,1)S(1)} %fusion.94), channel_id=1, source_target_pairs={{0,4},{2,6},{4,0},{6,2},{8,12},{10,14},{12,8},{14,10},{1,5},{3,7},... | collective-permute-start | bytes 2359304 | tf_op jit(solution)/shard_map/ppermute | solution.py:86
  272.9 16.9 %copy-start.14 = (f32[4,128,3,512]{3,1,2,0:T(8,128)S(1)}, f32[4,128,3,512]{3,1,2,0:T(8,128)}, u32[]{:S(2)}) copy-start(f32[4,128,3,512]{3,1,2,0:T(8,128)} %copy-done.13) | copy-start | bytes 9437188
  275.4 16.9 %collective-permute-start.25 = (bf16[1,128,2,512]{3,2,1,0:T(2,128)(2,1)S(1)}, bf16[1,128,2,512]{3,2,1,0:T(2,128)(2,1)S(1)}, u32[]{:S(2)}, u32[]{:S(2)}) collective-permute-start(bf16[1,128,2,512]{3,2,1,0:T(2,128)(2,1)S(1)} %dynamic-slice_convert_fusion.6), channel_id=1, source_target_pairs={{0,8},{2,10},{4,12},{6,14},{8,0},{10,2},{12,4},{14,6},{1,9},{3,11}... | collective-permute-start | bytes 786440 | tf_op jit(solution)/shard_map/ppermute | solution.py:86
  289.9 19.7 %copy-start.1 = (bf16[512,1024]{1,0:T(8,128)(2,1)S(1)}, bf16[512,1024]{1,0:T(8,128)(2,1)}, u32[]{:S(2)}) copy-start(bf16[512,1024]{1,0:T(8,128)(2,1)} %param.26) | copy-start | bytes 3145732
  291.5 17.2 %collective-permute-start.16 = (bf16[1,128,3,512]{3,1,2,0:T(8,128)(2,1)S(1)}, bf16[1,128,3,512]{3,1,2,0:T(8,128)(2,1)S(1)}, u32[]{:S(2)}, u32[]{:S(2)}) collective-permute-start(bf16[1,128,3,512]{3,1,2,0:T(8,128)(2,1)S(1)} %dynamic-slice_convert_fusion.4), channel_id=1, source_target_pairs={{0,8},{2,10},{4,12},{6,14},{8,0},{10,2},{12,4},{14,6},{1,9},{3,11}... | collective-permute-start | bytes 1179656 | tf_op jit(solution)/shard_map/ppermute | solution.py:86
  (22 other events, 40.7 us)

commit v2 on v0

v2 whole, which is shorter than its diff:
```python
import functools

import jax
import jax.numpy as jnp
from jax import lax
from jax.experimental import pallas as pl
from jax.experimental.pallas import tpu as pltpu
from jax.sharding import PartitionSpec as P

HEAD_DIM = 128
KERNEL = 9
REACH = 128
EDGE = 16
HALO = REACH + EDGE
epsilon = 1e-05
f32 = jnp.float32
bf16 = jnp.bfloat16
contract_rows = (((0,), (0,)), ((), ()))
contract_cols = (((1,), (1,)), ((), ()))


def shape(dims, dtype):
    return jax.ShapeDtypeStruct(dims, dtype)


def by_rows(count, step, body, copies=1):
    while count % (step * copies):
        copies -= 1

    def turn(index, carry):
        for copy in range(copies):
            body(pl.multiple_of(index * (step * copies) + copy * step, step))
        return carry

    lax.fori_loop(0, count // (step * copies), turn, 0)


NORM_STEP, NORM_COPIES = 16, 8
CONV_COPIES = 4
DEEP_COPIES = 4
BACK_COPIES = 2


def normalized(values):
    center = jnp.mean(values, axis=-1, keepdims=True)
    centred = values - center
    inverse = lax.rsqrt(jnp.mean(centred * centred, axis=-1, keepdims=True) + epsilon)
    return centred * inverse, center, inverse


def dot(left, right, numbers=(((1,), (0,)), ((), ()))):
    return lax.dot_general(left, right, numbers, preferred_element_type=f32)


def pack(place_ref, x_ref, cot_ref, valid_ref, out_ref, flags_ref, sems):
    rows, model = x_ref.shape
    flags = pltpu.make_async_copy(valid_ref, flags_ref, sems.at[2])
    flags.start()
    for core in range(2):

        @pl.when(place_ref[1] == core)
        def _():
            edges = (x_ref, HALO, 0), (cot_ref, EDGE, HALO)
            copies = [
                pltpu.make_async_copy(
                    ref.at[pl.ds(0 if core else rows - count, count)], out_ref.at[pl.ds(first, count)], sems.at[i]
                )
                for i, (ref, count, first) in enumerate(edges)
            ]
            for copy in copies:
                copy.start()
            out_ref[HALO + EDGE :] = jnp.zeros((EDGE, model), bf16)
            for copy in copies:
                copy.wait()

    flags.wait()
    out_ref[HALO + EDGE :, :rows] = jnp.broadcast_to(flags_ref[...].astype(f32), (EDGE, rows)).astype(bf16)


def project_own(x_ref, gain_ref, w_ref, attn_ref, out_ref, center_ref, inverse_ref):
    @pl.when(pl.program_id(0) == 0)
    def _():
        def norm_rows(row):
            normed, center, inverse = normalized(x_ref[pl.ds(row, NORM_STEP), :].astype(f32))
            attn_ref[pl.ds(row, NORM_STEP), :] = (normed * gain_ref[...]).astype(bf16)
            center_ref[pl.ds(row, NORM_STEP), :] = center
            inverse_ref[pl.ds(row, NORM_STEP), :] = inverse

        by_rows(x_ref.shape[0], NORM_STEP, norm_rows, NORM_COPIES)

    out_ref[0] = dot(attn_ref[...], w_ref[0]).astype(bf16)


def project_halo(place_ref, mine_ref, other_ref, gain_ref, w_ref, out_ref, attn_ref):
    @pl.when(pl.program_id(0) == 0)
    def _():
        for side, x_ref in enumerate((mine_ref, other_ref)):
            first = jnp.where(place_ref[1] == side, 0, HALO)

            def norm_rows(row):
                normed, _, _ = normalized(x_ref[pl.ds(row, 16), :].astype(f32))
                attn_ref[pl.ds(pl.multiple_of(row + first, 16), 16), :] = (normed * gain_ref[...]).astype(bf16)

            by_rows(HALO, 16, norm_rows, NORM_COPIES)

    out_ref[0] = dot(attn_ref[...], w_ref[0]).astype(bf16)


def attend(
    place_ref, own_ref, halo_ref, mine_ref, other_ref, own_valid_ref, w_ref, attended_ref, partial_ref, probs_ref, valid_ref, edge_ref, k_ref, v_ref, bias_ref,
):
    rows, width = own_ref.shape[1:]
    heads, blocks = width // HEAD_DIM, rows // REACH
    span = 3 * REACH
    scale = HEAD_DIM ** (-0.5)
    for which, ref in ((1, k_ref), (2, v_ref)):
        ref[:HALO] = halo_ref[which, :HALO]
        ref[HALO : HALO + rows] = own_ref[which]
        ref[HALO + rows :] = halo_ref[which, HALO:]

    def turned(row, first, last):
        chunks = range(first // REACH, -(-last // REACH))
        wide = [jnp.concatenate([row[:, c * REACH : (c + 1) * REACH]] * (REACH // 8), axis=0).T for c in chunks]
        start = first - first // REACH * REACH
        return jnp.concatenate(wide, axis=0)[start : start + last - first]

    flags = [ref[HALO + EDGE : HALO + 2 * EDGE, :rows].astype(f32)[:8] for ref in (mine_ref, other_ref)]
    low, high = jnp.where(place_ref[1] == 0, *flags), jnp.where(place_ref[1] == 0, *flags[::-1])
    valid_ref[:HALO] = turned(low, rows - HALO, rows)
    valid_ref[HALO : HALO + rows] = turned(jnp.broadcast_to(own_valid_ref[...].astype(f32), (8, rows)), 0, rows)
    valid_ref[HALO + rows : 2 * HALO + rows] = turned(high, 0, HALO)

    def set_bias(first_query, first_key, count):
        key = lax.broadcasted_iota(jnp.int32, (span, count), 0) + first_key
        query = lax.broadcasted_iota(jnp.int32, (span, count), 1) + first_query
        offset = key - query
        valid = valid_ref[pl.ds(first_key, span), :] > 0
        allowed = (jnp.abs(offset) <= REACH) & (valid | (offset == 0))
        bias_ref[:, :count] = jnp.where(allowed, 0.0, -jnp.inf)

    def block(queries, head, first_key, count):
        lanes = slice(head * HEAD_DIM, (head + 1) * HEAD_DIM)
        keys = k_ref[pl.ds(first_key, span), lanes]
        scores = dot(keys, queries, contract_cols) * scale + bias_ref[:, :count]
        highest = jnp.max(scores, axis=0, keepdims=True)
        raised = jnp.exp(scores - highest)
        probs = (raised * (1.0 / jnp.sum(raised, axis=0, keepdims=True))).astype(bf16)
        out = dot(probs, v_ref[pl.ds(first_key, span), lanes], contract_rows)
        return probs, out.astype(bf16)

    def turn(index, carry):
        first = pl.multiple_of(index * REACH, REACH)
        first_key = pl.multiple_of(first + EDGE, 16)
        set_bias(first + HALO, first_key, REACH)
        for head in range(heads):
            lanes = slice(head * HEAD_DIM, (head + 1) * HEAD_DIM)
            probs, out = block(own_ref[0, pl.ds(first, REACH), lanes], head, first_key, REACH)
            probs_ref[head, index] = probs
            attended_ref[pl.ds(pl.multiple_of(first + EDGE, 16), REACH), lanes] = out
        return carry

    lax.fori_loop(0, blocks, turn, 0)
    reach = REACH + HALO
    packs = [(side, head) for side in range(2) for head in range(heads)]
    starts = (HALO - EDGE, HALO)
    edge_ref[...] = jnp.zeros_like(edge_ref)
    for place, (side, head) in enumerate(packs):
        lanes = slice(head * HEAD_DIM, (head + 1) * HEAD_DIM)
        edge_ref[place * EDGE : (place + 1) * EDGE, lanes] = halo_ref[0, starts[side] : starts[side] + EDGE, lanes]
    count = len(packs) * EDGE
    lane = lax.broadcasted_iota(jnp.int32, (reach, count), 1)
    query = lane % EDGE + jnp.where(lane < heads * EDGE, REACH, HALO + rows)
    keys = (0, reach), (2 * HALO + rows - reach, 2 * HALO + rows)
    scores = []
    for first, last in keys:
        offset = lax.broadcasted_iota(jnp.int32, (reach, count), 0) + first - query
        allowed = (jnp.abs(offset) <= REACH) & ((valid_ref[first:last, :1] > 0) | (offset == 0))
        score = dot(k_ref[first:last], edge_ref[...], contract_cols) * scale
        scores.append(jnp.where(allowed, score, -jnp.inf))
    highest = jnp.maximum(*(jnp.max(score, axis=0, keepdims=True) for score in scores))
    raised = [jnp.exp(score - highest) for score in scores]
    inverse = 1.0 / sum(jnp.sum(part, axis=0, keepdims=True) for part in raised)
    out = sum(
        dot((part * inverse).astype(bf16), v_ref[first:last], contract_rows) for part, (first, last) in zip(raised, keys)
    ).astype(bf16)
    for place, (side, head) in enumerate(packs):
        lanes = slice(head * HEAD_DIM, (head + 1) * HEAD_DIM)
        first = side * (EDGE + rows)
        attended_ref[first : first + EDGE, lanes] = out[place * EDGE : (place + 1) * EDGE, lanes]
    partial_ref[...] = dot(attended_ref[...], w_ref[...]).astype(bf16)


def attend_back(own_ref, halo_ref, probs_ref, upstream_ref, dq_ref, dkv_ref, low_ref, high_ref, k_ref, v_ref, dk_ref, dv_ref):
    rows, width = own_ref.shape[1:]
    heads, blocks = width // HEAD_DIM, rows // REACH
    span = 3 * REACH
    scale = HEAD_DIM ** (-0.5)
    for which, ref in ((1, k_ref), (2, v_ref)):
        ref[:REACH] = halo_ref[which, EDGE:HALO]
        ref[REACH : REACH + rows] = own_ref[which]
        ref[REACH + rows :] = halo_ref[which, HALO : HALO + REACH]
    dk_ref[...] = jnp.zeros_like(dk_ref)
    dv_ref[...] = jnp.zeros_like(dv_ref)

    def turn(index, carry):
        first = pl.multiple_of(index * REACH, REACH)
        mine = pl.ds(first, REACH)
        window = pl.ds(first, span)
        for head in range(heads):
            lanes = slice(head * HEAD_DIM, (head + 1) * HEAD_DIM)
            upstream = upstream_ref[mine, lanes]
            rounded = probs_ref[head, index]
            probs = rounded.astype(f32)
            slopes = dot(v_ref[window, lanes], upstream, contract_cols)
            spread = jnp.sum(probs * slopes, axis=0, keepdims=True)
            grads = (probs * (slopes - spread) * scale).astype(bf16)
            dq_ref[0, mine, lanes] = dot(grads, k_ref[window, lanes], contract_rows).astype(bf16)
            dk_ref[window, lanes] += dot(grads, own_ref[0, mine, lanes])
            dv_ref[window, lanes] += dot(rounded, upstream)
        return carry

    lax.fori_loop(0, blocks, turn, 0)
    for which, ref in ((0, dk_ref), (1, dv_ref)):
        dkv_ref[which] = ref[REACH : REACH + rows]
        low_ref[which] = ref[:REACH].astype(bf16)
        high_ref[which] = ref[REACH + rows :].astype(bf16)


def convolve(
    place_ref, x_ref, mine_ref, other_side_ref, own_ref, other_ref, mask_ref, gain_ref, w_ref, taps_ref, w_out_ref,
    cot_ref,
    hidden_ref, conv_in_ref, acted_ref, partial_ref, lifted_grad_ref, norm_grad_ref, taps_grad_ref, center_ref, inverse_ref,
    conv_ext_ref, linear_ref, gate_ref, gated_ref, deep_ref, acted_grad_ref, cot_ext_ref,
):
    rows, _ = x_ref.shape
    width = taps_ref.shape[1]
    total = rows + 2 * EDGE
    half = (KERNEL - 1) // 2
    gain = gain_ref[...]

    def norm_rows(row, x, own_row):
        place = pl.multiple_of(row, 16)
        hidden = x.astype(f32) + (own_ref[pl.ds(place, 16), :].astype(f32) + other_ref[pl.ds(place, 16), :].astype(f32))
        normed, center, inverse = normalized(hidden)
        conv_in = (normed * gain).astype(bf16)
        conv_ext_ref[pl.ds(place, 16), :] = conv_in
        if own_row is not None:
            hidden_ref[pl.ds(own_row, 16), :] = hidden
            conv_in_ref[pl.ds(own_row, 16), :] = conv_in
            center_ref[pl.ds(own_row, 16), :] = center
            inverse_ref[pl.ds(own_row, 16), :] = inverse


    def chosen(side, rows):
        first = place_ref[1] == side
        return jnp.where(first, mine_ref[rows].astype(f32), other_side_ref[rows].astype(f32)).astype(bf16)

    norm_rows(0, chosen(0, slice(REACH, HALO)), None)
    by_rows(rows, 16, lambda row: norm_rows(row + EDGE, x_ref[pl.ds(row, 16), :], row), NORM_COPIES)
    norm_rows(EDGE + rows, chosen(1, slice(0, EDGE)), None)
    cot_ext_ref[:EDGE] = chosen(0, slice(HALO, HALO + EDGE))
    cot_ext_ref[EDGE : EDGE + rows] = cot_ref[...]
    cot_ext_ref[EDGE + rows :] = chosen(1, slice(HALO, HALO + EDGE))
    linear_ref[...] = dot(conv_ext_ref[...], w_ref[0])
    gate_ref[...] = dot(conv_ext_ref[...], w_ref[1])
    acted_grad_ref[...] = dot(cot_ext_ref[...], w_out_ref[...], contract_cols)

    def mask_rows(row, count):
        values = mask_ref[pl.ds(pl.multiple_of(row + REACH, 8), count), :]
        return jnp.concatenate([values] * (width // REACH), axis=1)

    def gate_rows(row):
        here = pl.ds(row, 16)
        gate = jax.nn.sigmoid(gate_ref[here, :])
        gate_ref[here, :] = gate
        gated_ref[here, :] = (linear_ref[here, :] * gate * mask_rows(row, 16)).astype(bf16).astype(f32)

    by_rows(total, 16, gate_rows, CONV_COPIES)
    taps = [taps_ref[t : t + 1, :] for t in range(KERNEL)]

    def deep_rows(row, count, own_row):
        around = gated_ref[pl.ds(pl.multiple_of(row - 8, 8), count + 16), :]
        deep = taps[0] * around[8 - half : 8 - half + count]
        for t in range(1, KERNEL):
            deep = deep + taps[t] * around[8 - half + t : 8 - half + t + count]
        here = pl.ds(row, count)
        sig = jax.nn.sigmoid(deep)
        if own_row is not None:
            acted_ref[pl.ds(own_row, count), :] = (deep * sig).astype(bf16)
        acted_grad = acted_grad_ref[here, :].astype(bf16).astype(f32)
        deep_ref[here, :] = (acted_grad * (sig * (1.0 + deep * (1.0 - sig)))).astype(bf16).astype(f32)

    deep_rows(8, 8, None)
    by_rows(rows, 16, lambda row: deep_rows(pl.multiple_of(row + EDGE, 16), 16, row), DEEP_COPIES)
    deep_rows(EDGE + rows, 8, None)
    partial_ref[...] = dot(acted_ref[...], w_out_ref[...]).astype(bf16)

    def back_rows(row, sums):
        center = pl.multiple_of(row + EDGE, 16)
        here = pl.ds(center, 16)
        above = pl.ds(pl.multiple_of(center - 8, 8), 32)
        around, values = deep_ref[above, :], gated_ref[above, :]
        deep_grad = around[8:24]
        grad = taps[0] * around[8 + half : 24 + half]
        for t in range(1, KERNEL):
            grad = grad + taps[t] * around[8 + half - t : 24 + half - t]
        products = (deep_grad * values[8 - half + t : 24 - half + t] for t in range(KERNEL))
        sums = tuple(total_t + (product[:8] + product[8:]) for total_t, product in zip(sums, products))
        gate, linear = gate_ref[here, :], linear_ref[here, :]
        grad = grad * mask_rows(center, 16)
        lifted_grad_ref[0, pl.ds(row, 16), :] = (grad * gate).astype(bf16)
        lifted_grad_ref[1, pl.ds(row, 16), :] = (grad * linear * gate * (1.0 - gate)).astype(bf16)
        return sums

    def back_turn(index, sums):
        for copy in range(BACK_COPIES):
            sums = back_rows(pl.multiple_of(index * (16 * BACK_COPIES) + 16 * copy, 16), sums)
        return sums

    zero = jnp.zeros((8, width), f32)
    sums = lax.fori_loop(0, rows // (16 * BACK_COPIES), back_turn, (zero,) * KERNEL)
    for t in range(KERNEL):
        taps_grad_ref[t : t + 1, :] = jnp.sum(sums[t], axis=0, keepdims=True)
    norm_grad_ref[...] = (
        dot(lifted_grad_ref[0], w_ref[0], contract_cols) + dot(lifted_grad_ref[1], w_ref[1], contract_cols)
    ).astype(bf16)


def norm_back(source_ref, center_ref, inverse_ref, base_ref, own_ref, other_ref, gain_ref, w_ref, grad_ref, rounded_ref, gain_grad_ref, attended_grad_ref):
    gain = gain_ref[...]
    rows, model = source_ref.shape

    def back_rows(row, total):
        here = pl.ds(row, 16)
        inverse = inverse_ref[here, :]
        normed = (source_ref[here, :].astype(f32) - center_ref[here, :]) * inverse
        upstream = own_ref[here, :].astype(f32) + other_ref[here, :].astype(f32)
        scaled = upstream * gain
        first = jnp.mean(scaled, axis=-1, keepdims=True)
        second = jnp.mean(scaled * normed, axis=-1, keepdims=True)
        grad = base_ref[here, :].astype(f32) + inverse * (scaled - first - normed * second)
        if grad_ref is not None:
            grad_ref[here, :] = grad
        rounded_ref[here, :] = grad.astype(bf16)
        product = upstream * normed
        return total + (product[:8] + product[8:])

    def turn(index, total):
        for copy in range(NORM_COPIES):
            total = back_rows(pl.multiple_of(index * (16 * NORM_COPIES) + 16 * copy, 16), total)
        return total

    total = lax.fori_loop(0, rows // (16 * NORM_COPIES), turn, jnp.zeros((8, model), f32))
    gain_grad_ref[...] = jnp.sum(total, axis=0, keepdims=True)
    if w_ref is not None:
        attended_grad_ref[...] = dot(rounded_ref[...], w_ref[...], contract_cols).astype(bf16)


def norm_back_last(
    devices, place_ref, source_ref, center_ref, inverse_ref, base_ref, own_ref, other_ref, gain_ref, gain_conv_ref, taps_ref,
    rounded_ref, sent_ref, kept_ref, gain_grad_ref,
):
    norm_back(source_ref, center_ref, inverse_ref, base_ref, own_ref, other_ref, gain_ref, None, None, rounded_ref, gain_grad_ref, None)
    gain_part, tap_part = gain_grad_ref.shape[1] // devices, taps_ref.shape[1] // devices
    for side in range(2):

        @pl.when(place_ref[0] % 2 == side)
        def _():
            for chunk in range(devices):
                out_ref = kept_ref if chunk % 2 == side else sent_ref
                first = chunk // 2 * EDGE
                out_ref[0, first : first + EDGE] = jnp.zeros((EDGE, out_ref.shape[2]), f32)
                out_ref[0, first : first + KERNEL, :tap_part] = taps_ref[:, chunk * tap_part : (chunk + 1) * tap_part]
                lanes = slice(chunk * gain_part, (chunk + 1) * gain_part)
                out_ref[0, first + KERNEL : first + KERNEL + 1, :gain_part] = gain_conv_ref[:, lanes]
                out_ref[0, first + KERNEL + 1 : first + KERNEL + 2, :gain_part] = gain_grad_ref[:, lanes]


def bits_of(devices):
    return [1 << i for i in range(devices.bit_length() - 1)]


def placed(chunk, bit):
    return (chunk // (2 * bit)) * bit + chunk % bit


def weight_grad(devices, lefts, groups, rims, place_ref, *refs):
    rights = sorted({right for _, pieces in groups for _, right, _, _ in pieces})
    left_refs, refs = refs[:lefts], refs[lefts:]
    right_refs, refs = list(refs[: len(rights)]), refs[len(rights) :]
    rows = left_refs[0].shape[0]
    if rims:
        low_ref, high_ref, *refs = refs
    halves, refs = refs[: 2 * len(groups)], refs[2 * len(groups) :]
    if rims:
        sum_ref, *refs = refs
        source = right_refs[-1]
        for piece in range(source.shape[0]):
            sum_ref[piece, :REACH] = (source[piece, :REACH] + low_ref[piece].astype(f32)).astype(bf16)
            sum_ref[piece, REACH : rows - REACH] = source[piece, REACH : rows - REACH].astype(bf16)
            sum_ref[piece, rows - REACH :] = (source[piece, rows - REACH :] + high_ref[piece].astype(f32)).astype(bf16)
        right_refs[-1] = sum_ref
    *turned_refs, result_ref = refs
    part = left_refs[0].shape[1] // devices
    for left_ref, turned_ref in zip(left_refs, turned_refs):
        turned_ref[...] = left_ref[...].T
    for group, (bit, pieces) in enumerate(groups):
        for slot, (left, right, index, first) in enumerate(pieces):
            result_ref[...] = dot(turned_refs[left][...], right_refs[right][index, first : first + rows]).astype(bf16)
            for side in range(2):

                @pl.when((place_ref[0] // bit) % 2 == side)
                def _():
                    for chunk in range(devices):
                        out_ref = halves[2 * group + ((chunk // bit) % 2 == side)]
                        where = slice(placed(chunk, bit) * part, (placed(chunk, bit) + 1) * part)
                        out_ref[slot, where] = result_ref[chunk * part : (chunk + 1) * part]


def call_weight_grad(place, lefts, rights, groups, name, rims=()):
    rows, model = lefts[0].shape
    width = rights[0].shape[-1]
    vmem = pl.BlockSpec(memory_space=pltpu.VMEM)
    summed = (shape(rights[-1].shape, bf16),) if rims else ()
    halves = [shape((len(pieces), model // 2, width), bf16) for _, pieces in groups for _ in range(2)]
    outs = kernel(
        functools.partial(weight_grad, lax.axis_size("tm"), len(lefts), groups, bool(rims)),
        name,
        out_shape=tuple(halves) + summed,
        in_specs=[pl.BlockSpec(memory_space=pltpu.SMEM)] + [vmem] * (len(lefts) + len(rights) + len(rims)),
        scratch_shapes=[pltpu.VMEM((model, rows), bf16) for _ in lefts] + [pltpu.VMEM((model, width), bf16)],
    )(place, *lefts, *rights, *rims)
    return [outs[2 * i : 2 * i + 2] for i in range(len(groups))] + list(outs[2 * len(groups) :])


def swapped(array, bit):
    devices = lax.axis_size("tm")
    return lax.ppermute(array, "tm", [(i, i ^ bit) for i in range(devices)])


def fold(before, after, bit, place_ref, got_ref, kept_ref, sent_ref, keep_ref):
    part = got_ref.shape[1] // (2 * before * after)
    for side in range(2):

        @pl.when((place_ref[0] // bit) % 2 == side)
        def _():
            for piece in range(got_ref.shape[0]):
                for block in range(2 * before):
                    rows = slice(block * after * part, (block + 1) * after * part)
                    total = kept_ref[piece, rows].astype(f32) + got_ref[piece, rows].astype(f32)
                    out_ref = keep_ref if block % 2 == side else sent_ref
                    there = slice(block // 2 * after * part, (block // 2 + 1) * after * part)
                    out_ref[piece, there] = total.astype(out_ref.dtype)


def halved(place, halves, order, name):
    sent, kept = halves
    layout = sorted(order, reverse=True)
    vmem = pl.BlockSpec(memory_space=pltpu.VMEM)
    for step, bit in enumerate(order):
        got = swapped(sent, bit)
        layout.remove(bit)
        if not layout:
            return kept.astype(f32) + got.astype(f32)
        bit = order[step + 1]
        before = 1 << layout.index(bit)
        after = (1 << len(layout)) // (2 * before)
        pieces, rows, width = kept.shape
        sent, kept = kernel(
            functools.partial(fold, before, after, bit),
            f"fold_{name}{step + 1}",
            out_shape=(shape((pieces, rows // 2, width), kept.dtype),) * 2,
            in_specs=[pl.BlockSpec(memory_space=pltpu.SMEM), vmem, vmem],
        )(place, got, kept)


def toward_sides(array):
    devices = lax.axis_size("tm")
    up = [(2 * i, 2 * i + 2) for i in range(devices - 1)]
    down = [(2 * i + 3, 2 * i + 1) for i in range(devices - 1)]
    return lax.ppermute(array, ("tm", "mp"), up + down)


def partner(array):
    return lax.ppermute(array, "mp", [(0, 1), (1, 0)])


def from_sides(to_next, to_previous):
    devices = lax.axis_size("tm")
    up = [(i, i + 1) for i in range(devices - 1)]
    down = [(j, i) for i, j in up]
    low = lax.ppermute(to_next, "tm", up)
    high = lax.ppermute(to_previous, "tm", down)
    return low, high


VMEM_MIB = dict(
    pack=3, project_own=8, project_halo=8, attend=12, convolve=24, norm_back=11, attend_back=13, input_grad=8,
    norm_back_last=10, output=8, grad_conv=16, grad_attn=20,
)
FOLD_MIB = 4


def kernel(function, name, **options):
    limit = pltpu.CompilerParams(vmem_limit_bytes=VMEM_MIB.get(name, FOLD_MIB) << 20)
    return pl.pallas_call(function, compiler_params=limit, **options)


def layer(
    frames, valid, w_qkv, w_out, gain_attn, w_conv_in, w_depth, gain_conv, w_conv_out, cotangent
):
    rows, model = frames.shape
    width = w_out.shape[0]
    heads, blocks = width // HEAD_DIM, rows // REACH
    devices = lax.axis_size("tm")
    span = 3 * REACH
    total = rows + 2 * EDGE
    window = rows + 2 * HALO
    smem, vmem = pl.BlockSpec(memory_space=pltpu.SMEM), pl.BlockSpec(memory_space=pltpu.VMEM)
    gain_a, gain_c = gain_attn.reshape(1, model), gain_conv.reshape(1, model)

    place = jnp.stack([lax.axis_index("tm"), lax.axis_index("mp")])
    valid_row = valid.reshape(1, rows)
    mine = kernel(
        pack,
        "pack",
        out_shape=shape((HALO + 2 * EDGE, model), bf16),
        in_specs=[smem] + [pl.BlockSpec(memory_space=pltpu.HBM)] * 3,
        out_specs=vmem,
        scratch_shapes=[pltpu.VMEM((1, rows), jnp.int32), pltpu.SemaphoreType.DMA((3,))],
    )(place, *(pltpu.with_memory_space_constraint(a, pltpu.HBM) for a in (frames, cotangent, valid_row)))
    mine = toward_sides(mine)
    other = partner(mine)
    w3 = jnp.transpose(w_qkv, (1, 0, 2))
    w2 = jnp.transpose(w_conv_in, (1, 0, 2))

    attn_in, own, attn_center, attn_inverse = kernel(
        project_own,
        "project_own",
        out_shape=(
            shape((rows, model), bf16), shape((3, rows, width), bf16), shape((rows, 1), f32), shape((rows, 1), f32)
        ),
        grid=(3,),
        in_specs=[
            pl.BlockSpec((rows, model), lambda s: (0, 0)),
            pl.BlockSpec((1, model), lambda s: (0, 0)),
            pl.BlockSpec((1, model, width), lambda s: (s, 0, 0)),
        ],
        out_specs=(
            pl.BlockSpec((rows, model), lambda s: (0, 0)),
            pl.BlockSpec((1, rows, width), lambda s: (s, 0, 0)),
            pl.BlockSpec((rows, 1), lambda s: (0, 0)),
            pl.BlockSpec((rows, 1), lambda s: (0, 0)),
        ),
    )(frames, gain_a, w3)
    own, w2 = lax.optimization_barrier((own, w2))
    halo = kernel(
        project_halo,
        "project_halo",
        out_shape=shape((3, 2 * HALO, width), bf16),
        grid=(3,),
        in_specs=[
            smem,
            pl.BlockSpec((HALO, model), lambda s: (0, 0)),
            pl.BlockSpec((HALO, model), lambda s: (0, 0)),
            pl.BlockSpec((1, model), lambda s: (0, 0)),
            pl.BlockSpec((1, model, width), lambda s: (s, 0, 0)),
        ],
        out_specs=pl.BlockSpec((1, 2 * HALO, width), lambda s: (s, 0, 0)),
        scratch_shapes=[pltpu.VMEM((2 * HALO, model), bf16)],
    )(place, mine, other, gain_a, w3)
    attended, own_partial, probs, mask_full = kernel(
        attend,
        "attend",
        out_shape=(
            shape((total, width), bf16),
            shape((total, model), bf16),
            shape((heads, blocks, span, REACH), bf16),
            shape((window, REACH), f32),
        ),
        scratch_shapes=[
            pltpu.VMEM((2 * heads * EDGE, width), bf16),
            pltpu.VMEM((window, width), bf16),
            pltpu.VMEM((window, width), bf16),
            pltpu.VMEM((span, REACH), f32),
        ],
        in_specs=[smem] + [vmem] * 6,
    )(place, own, halo, mine, other, valid_row, w_out)
    other_partial = partner(own_partial)

    whole = pl.BlockSpec(memory_space=pltpu.VMEM)
    hidden, conv_in, acted, out_partial, lifted_grad, norm_partial, taps_grad, center, inverse = kernel(
        convolve,
        "convolve",
        out_shape=(
            shape((rows, model), f32),
            shape((rows, model), bf16),
            shape((rows, width), bf16),
            shape((rows, model), bf16),
            shape((2, rows, width), bf16),
            shape((rows, model), bf16),
            shape((KERNEL, width), f32),
            shape((rows, 1), f32),
            shape((rows, 1), f32),
        ),
        scratch_shapes=[
            pltpu.VMEM((total, model), bf16),
            pltpu.VMEM((total, width), f32),
            pltpu.VMEM((total, width), f32),
            pltpu.VMEM((total, width), f32),
            pltpu.VMEM((total, width), f32),
            pltpu.VMEM((total, width), f32),
            pltpu.VMEM((total, model), bf16),
        ],
        in_specs=[smem] + [vmem] * 11,
    )(place, frames, mine, other, own_partial, other_partial, mask_full, gain_c, w2, w_depth, w_conv_out, cotangent)
    norm_other = partner(norm_partial)
    bits = bits_of(devices)
    late = bits[1:] + bits[:1]
    early = bits[0]
    conv_out, linear, gate = (early, [(0, 0, 0, 0)]), (early, [(1, 1, 0, 0)]), (late[0], [(1, 1, 1, 0)])
    conv_out_halves, linear_halves, gate_halves = call_weight_grad(
        place, [cotangent, conv_in], [acted[None], lifted_grad], [conv_out, linear, gate], "grad_conv"
    )

    grad_hidden, hidden_grad_b, gain_conv_local, attended_grad = kernel(
        norm_back,
        "norm_back",
        out_shape=(
            shape((rows, model), f32),
            shape((rows, model), bf16),
            shape((1, model), f32),
            shape((rows, width), bf16),
        ),
    )(hidden, center, inverse, cotangent, norm_partial, norm_other, gain_c, w_out)
    dq, dkv, low_sent, high_sent = kernel(
        attend_back,
        "attend_back",
        out_shape=(
            shape((1, rows, width), bf16),
            shape((2, rows, width), f32),
            shape((2, REACH, width), bf16),
            shape((2, REACH, width), bf16),
        ),
        scratch_shapes=[
            pltpu.VMEM((rows + 2 * REACH, width), bf16),
            pltpu.VMEM((rows + 2 * REACH, width), bf16),
            pltpu.VMEM((rows + 2 * REACH, width), f32),
            pltpu.VMEM((rows + 2 * REACH, width), f32),
        ],
    )(own, halo, probs, attended_grad)
    low_rim, high_rim = from_sides(high_sent, low_sent)
    value, query_proj, key = (
        (late[0], [(0, 2, 1, 0)]),
        (early, [(0, 0, 0, 0), (1, 1, 0, EDGE)]),
        (early, [(0, 2, 0, 0)]),
    )
    value_halves, query_proj_halves, key_halves, dkv = call_weight_grad(
        place,
        [attn_in, hidden_grad_b],
        [dq, attended[None], dkv],
        [value, query_proj, key],
        "grad_attn",
        rims=(low_rim, high_rim),
    )

    def input_grad(q_ref, kv_ref, w_ref, out_ref):
        out_ref[...] = (
            dot(q_ref[0], w_ref[0], contract_cols)
            + dot(kv_ref[0], w_ref[1], contract_cols)
            + dot(kv_ref[1], w_ref[2], contract_cols)
        ).astype(bf16)

    attn_partial = kernel(input_grad, "input_grad", out_shape=shape((rows, model), bf16))(dq, dkv, w3)
    attn_other = partner(attn_partial)
    grad_frames, *small_halves = kernel(
        functools.partial(norm_back_last, devices),
        "norm_back_last",
        out_shape=(shape((rows, model), bf16),) + (shape((1, devices // 2 * EDGE, REACH), f32),) * 2,
        in_specs=[smem] + [vmem] * 9,
        scratch_shapes=[pltpu.VMEM((1, model), f32)],
    )(place, frames, attn_center, attn_inverse, grad_hidden, attn_partial, attn_other, gain_a, gain_conv_local, taps_grad)

    out_other = partner(out_partial)

    def output_rows(hidden_ref, own_ref, other_ref, out_ref):
        out_ref[...] = (hidden_ref[...] + (own_ref[...].astype(f32) + other_ref[...].astype(f32))).astype(bf16)

    output = kernel(output_rows, "output", out_shape=shape((rows, model), bf16))(hidden, out_partial, out_other)

    grad_conv_out = halved(place, conv_out_halves, bits, "rco")[0].T
    grad_linear = halved(place, linear_halves, bits, "rl")
    grad_gate = halved(place, gate_halves, late, "rg")
    grad_value = halved(place, value_halves, late, "rv")
    grad_query_proj = halved(place, query_proj_halves, bits, "rqp")
    grad_key = halved(place, key_halves, bits, "rk")
    grad_proj = grad_query_proj[1].T
    grad_conv_in = jnp.stack([grad_linear[0], grad_gate[0]], axis=1)
    grad_qkv = jnp.transpose(jnp.concatenate([grad_query_proj[:1], grad_key, grad_value]), (1, 0, 2))
    tap_part, gain_part = width // devices, model // devices
    small = halved(place, small_halves, bits, "small")[0]
    grad_depth = small[:KERNEL, :tap_part]
    grad_gain_conv = small[KERNEL, :gain_part]
    grad_gain_attn = small[KERNEL + 1, :gain_part]
    return (
        output,
        grad_frames,
        grad_qkv,
        grad_proj,
        grad_gain_attn,
        grad_conv_in,
        grad_depth,
        grad_conv_out,
        grad_gain_conv,
    )


def solution(mesh):
    return jax.shard_map(
        layer,
        mesh=mesh,
        in_specs=(
            P(("groups", "tm"), None),
            P(("groups", "tm")),
            P(None, None, "mp"),
            P("mp", None),
            P(),
            P(None, None, "mp"),
            P(None, "mp"),
            P(),
            P("mp", None),
            P(("groups", "tm"), None),
        ),
        out_specs=(
            P(("groups", "tm"), None),
            P(("groups", "tm"), None),
            P(("groups", "tm"), None, "mp"),
            P(("groups", "mp"), "tm"),
            P(("groups", "tm")),
            P(("groups", "tm"), None, "mp"),
            P("groups", ("mp", "tm")),
            P(("groups", "mp"), "tm"),
            P(("groups", "tm")),
        ),
        check_vma=False,
    )
```

time: 531 us -> 178 us (0.34); the launches traced: 523 us -> 177 us
  waiting for transfers between devices: 295 us -> 67.8 us
  matrix products: 85 us -> 0 us
  Pallas kernels: 0 us -> 61 us
  other arithmetic: 41.2 us -> 2.86 us
  local copies, waits for them, and re-layouts: 35.9 us -> 5.38 us
  blocking collectives: 22 us -> 0 us
  between operations: 16 us -> 1.09 us
  starting transfers between devices: 28 us -> 38.9 us
    reduce_scatter x2 -> x0, waiting for transfers between devices: 118 us -> none  [the longest x1 69 us: local(): lax.psum_scatter(conv_in_local.astype(jnp.bfloat16), 'tm', scatter_dimens...]
    unnamed x11 -> x0, waiting for transfers between devices: 113 us -> none
    dot_general x18 -> x0, matrix products: 85 us -> none  [the longest x1 18.2 us: local(): jnp.einsum('hqk,khd->qhd', grad_scores, window[:, 0], preferred_element_t...]
    pallas_call x0 -> x26, Pallas kernels: none -> 61 us  [the longest x14 12.6 us: halved(): kernel(functools.partial(fold, before, after, bit), f'fold_{name}{step +...]
    ppermute x10 -> x29, waiting for transfers between devices: 12.9 us -> 67.8 us  [the longest x21 38.6 us: swapped(): return lax.ppermute(array, 'tm', [(i, i ^ bit) for i in range(devices)])]
    psum x3 -> x0, waiting for transfers between devices: 51.5 us -> none  [model_sum(): return lax.psum(partial_sum, 'mp')]
    unnamed x84 -> x34, local copies, waits for them, and re-layouts: 27 us -> 4.83 us
    unnamed x1 -> x0, blocking collectives: 22 us -> none
  transfers between devices with their start and end apart: 18 -> 29, of which waited for: 11 -> 11; matrix products, arithmetic and copies ran while one was open for 22% -> 3% of each run, Pallas kernels for 0% -> 22%
where the time goes in v2:
time: 178 us; the launch traced here: 177 us
  waiting for transfers between devices  67.8 us (38%)
  Pallas kernels  61 us (34%)
  starting transfers between devices  38.9 us (22%)
  local copies, waits for them, and re-layouts  5.38 us (3%)
  other arithmetic  2.86 us (2%)
    ppermute x21, waiting for transfers between devices, swapped(): return lax.ppermute(array, 'tm', [(i, i ^ bit) for i in range(devices)])  38.6 us
    ppermute x21, starting transfers between devices, swapped(): return lax.ppermute(array, 'tm', [(i, i ^ bit) for i in range(devices)])  27.3 us
    ppermute x1, waiting for transfers between devices, from_sides(): low = lax.ppermute(to_next, 'tm', up)  18.3 us
    pallas_call x14, Pallas kernels, halved(): kernel(functools.partial(fold, before, after, bit), f'fold_{name}{step +...  12.6 us
    pallas_call x1, Pallas kernels, layer(): kernel(convolve, 'convolve', out_shape=(shape((rows, model), f32), shape(...  12.4 us
    ppermute x1, waiting for transfers between devices, toward_sides(): return lax.ppermute(array, ('tm', 'mp'), up + down)  8.53 us
    pallas_call x2, Pallas kernels, call_weight_grad(): kernel(functools.partial(weight_grad, lax.axis_size('tm'), len(lefts), gr...  6.64 us
    pallas_call x1, Pallas kernels, layer(): kernel(attend_back, 'attend_back', out_shape=(shape((1, rows, width), bf1...  5.87 us
  transfers between devices with their start and end apart: 29, of which 11 were waited for; matrix products, arithmetic and copies ran while one was open for 3% of the time, Pallas kernels for 22%

profile of v2, /device:TPU:0, one launch (start us, length us, event | category | flops | bytes accessed | tf_op | source)
XLA Modules:
  0.0 177.2 jit_solution(18264173719870513643)
XLA Ops:
  0.7 1.6 shard_map.169
  2.3 5.2 %collective-permute-start = (bf16[176,1024]{1,0:T(8,128)(2,1)S(1)}, bf16[176,1024]{1,0:T(8,128)(2,1)S(1)}, u32[]{:S(2)}, u32[]{:S(2)}) collective-permute-start(bf16[176,1024]{1,0:T(8,128)(2,1)S(1)} %shard_map.169), channel_id=1, source_target_pairs={{0,2},{2,4},{4,6},{6,8},{8,10},{10,12},{12,14},{3,1},{5,3},{7,5},{... | collective-permute-start | bytes 1081352 | tf_op jit(solution)/shard_map/ppermute | solution.py:481
  7.5 8.5 %collective-permute-done.mine_ref = bf16[176,1024]{1,0:T(8,128)(2,1)S(1)} collective-permute-done((bf16[176,1024]{1,0:T(8,128)(2,1)S(1)}, bf16[176,1024]{1,0:T(8,128)(2,1)S(1)}, u32[]{:S(2)}, u32[]{:S(2)}) %collective-permute-start) | collective-permute-done | bytes 360480 | tf_op jit(solution)/shard_map/ppermute | solution.py:481
  16.4 3.2 %shard_map.170 = (bf16[512,1024]{1,0:T(8,128)(2,1)S(1)}, bf16[3,512,512]{2,1,0:T(8,128)(2,1)S(1)}, f32[512,1]{1,0:T(8,128)S(1)}, f32[512,1]{1,0:T(8,128)S(1)}) custom-call(bf16[512,1024]{1,0:T(8,128)(2,1)S(1)} %copy-done.1, f32[1,1024]{1,0:T(1,128)S(1)} %bitcast.37, bf16[3,1024,512]{2,1,0:T(8,128)(2,1)S(1)} %bitcast.31), custom_call_target="tpu_custom_call" | custom-call | tf_op jit(solution)/shard_map/pallas_call | solution.py:537
  19.7 3.2 %shard_map.171.halo_ref = bf16[3,288,512]{2,1,0:T(8,128)(2,1)S(1)} custom-call(s32[2]{0:T(128)S(1)} %pad_add_fusion.place_ref, bf16[176,1024]{1,0:T(8,128)(2,1)S(1)} %collective-permute-done.mine_ref, bf16[176,1024]{1,0:T(8,128)(2,1)S(1)} %collective-permute-done.1.other_ref.other_side_ref, f32[1,1024]{1,0:T(1,128)S(1)} %bitcast.38, ...), custom_call_target="tpu_custom_call" | custom-call | tf_op jit(solution)/shard_map/pallas_call | solution.py:557
  23.0 4.9 %shard_map.172 = (bf16[544,512]{1,0:T(8,128)(2,1)S(1)}, bf16[544,1024]{1,0:T(8,128)(2,1)S(1)}, bf16[4,4,384,128]{3,2,1,0:T(8,128)(2,1)S(1)}, f32[800,128]{1,0:T(8,128)S(1)}) custom-call(s32[2]{0:T(128)S(1)} %pad_add_fusion.place_ref, bf16[3,512,512]{2,1,0:T(8,128)(2,1)S(1)} %get-tuple-element.81.own_ref, bf16[3,288,512]{2,1,0:T(8,128)(2,1)S(1)} %shard_map.171.halo_ref, ...), custom_call_target="tpu_custom_call" | custom-call | tf_op jit(solution)/shard_map/pallas_call | solution.py:572
  27.9 0.6 collective-permute-start.2
  28.5 2.4 %collective-permute-done.2.other_ref = bf16[544,1024]{1,0:T(8,128)(2,1)S(1)} collective-permute-done((bf16[544,1024]{1,0:T(8,128)(2,1)S(1)}, bf16[544,1024]{1,0:T(8,128)(2,1)S(1)}, u32[]{:S(2)}, u32[]{:S(2)}) %collective-permute-start.2) | collective-permute-done | bytes 1114144 | tf_op jit(solution)/shard_map/ppermute | solution.py:485
  30.9 12.4 %shard_map.173 = (f32[512,1024]{1,0:T(8,128)S(1)}, bf16[512,1024]{1,0:T(8,128)(2,1)S(1)}, bf16[512,512]{1,0:T(8,128)(2,1)S(1)}, bf16[512,1024]{1,0:T(8,128)(2,1)...) custom-call(s32[2]{0:T(128)S(1)} %pad_add_fusion.place_ref, ...), custom_call_target="tpu_custom_call" | custom-call | tf_op jit(solution)/shard_map/pallas_call | solution.py:592
  43.7 2.9 %shard_map.188 = (bf16[1,512,512]{2,1,0:T(8,128)(2,1)S(1)}, bf16[1,512,512]{2,1,0:T(8,128)(2,1)S(1)}, bf16[1,512,512]{2,1,0:T(8,128)(2,1)S(1)}, bf16[1,512,512]{...) custom-call(s32[2]{0:T(128)S(1)} %pad_add_fusion.place_ref, ...), custom_call_target="tpu_custom_call" | custom-call | tf_op jit(solution)/shard_map/pallas_call | solution.py:426
  46.6 2.6 %collective-permute-start.20 = (bf16[1,512,512]{2,1,0:T(8,128)(2,1)S(1)}, bf16[1,512,512]{2,1,0:T(8,128)(2,1)S(1)}, u32[]{:S(2)}, u32[]{:S(2)}) collective-permute-start(bf16[1,512,512]{2,1,0:T(8,128)(2,1)S(1)} %get-tuple-element.133), channel_id=1, source_target_pairs={{0,2},{2,0},{4,6},{6,4},{8,10},{10,8},{12,14},{14,12},{1,3},{3,1},... | collective-permute-start | bytes 1572872 | tf_op jit(solution)/shard_map/ppermute | solution.py:438
  49.1 1.6 collective-permute-start.23
  50.8 2.7 %shard_map.175 = (f32[512,1024]{1,0:T(8,128)S(1)}, bf16[512,1024]{1,0:T(8,128)(2,1)S(1)}, f32[1,1024]{1,0:T(1,128)S(1)}, bf16[512,512]{1,0:T(8,128)(2,1)S(1)}) custom-call(f32[512,1024]{1,0:T(8,128)S(1)} %get-tuple-element.85.hidden_ref.source_ref, f32[512,1]{1,0:T(8,128)S(1)} %get-tuple-element.89.center_ref, f32[512,1]{1,0:T(8,128)S(1)} %get-tuple-element.90.inverse_ref, ...), custom_call_target="tpu_custom_call" | custom-call | tf_op jit(solution)/shard_map/pallas_call | solution.py:626
  53.6 5.9 %shard_map.176 = (bf16[1,512,512]{2,1,0:T(8,128)(2,1)S(1)}, f32[2,512,512]{2,1,0:T(8,128)S(1)}, bf16[2,128,512]{2,1,0:T(8,128)(2,1)S(1)}, bf16[2,128,512]{2,1,0:T(8,128)(2,1)S(1)}) custom-call(bf16[3,512,512]{2,1,0:T(8,128)(2,1)S(1)} %get-tuple-element.81.own_ref, bf16[3,288,512]{2,1,0:T(8,128)(2,1)S(1)} %shard_map.171.halo_ref, ...), custom_call_target="tpu_custom_call" | custom-call | tf_op jit(solution)/shard_map/pallas_call | solution.py:636
  59.4 3.9 %collective-permute-start.5 = (bf16[2,128,512]{2,1,0:T(8,128)(2,1)S(1)}, bf16[2,128,512]{2,1,0:T(8,128)(2,1)S(1)}, u32[]{:S(2)}, u32[]{:S(2)}) collective-permute-start(bf16[2,128,512]{2,1,0:T(8,128)(2,1)S(1)} %get-tuple-element.100), channel_id=1, source_target_pairs={{0,2},{2,4},{4,6},{6,8},{8,10},{10,12},{12,14},{1,3},{3,5},{5,7},{... | collective-permute-start | bytes 786440 | tf_op jit(solution)/shard_map/ppermute | solution.py:492
  63.3 1.5 collective-permute-start.6
  64.8 18.3 %collective-permute-done.5.refs_5_ = bf16[2,128,512]{2,1,0:T(8,128)(2,1)S(1)} collective-permute-done((bf16[2,128,512]{2,1,0:T(8,128)(2,1)S(1)}, bf16[2,128,512]{2,1,0:T(8,128)(2,1)S(1)}, u32[]{:S(2)}, u32[]{:S(2)}) %collective-permute-start.5) | collective-permute-done | bytes 262176 | tf_op jit(solution)/shard_map/ppermute | solution.py:492
  83.1 3.8 %shard_map.177 = (bf16[1,512,512]{2,1,0:T(8,128)(2,1)S(1)}, bf16[1,512,512]{2,1,0:T(8,128)(2,1)S(1)}, bf16[2,512,512]{2,1,0:T(8,128)(2,1)S(1)}, bf16[2,512,512]{...) custom-call(s32[2]{0:T(128)S(1)} %pad_add_fusion.place_ref, ...), custom_call_target="tpu_custom_call" | custom-call | tf_op jit(solution)/shard_map/pallas_call | solution.py:426
  86.9 2.6 %collective-permute-start.11 = (bf16[1,512,512]{2,1,0:T(8,128)(2,1)S(1)}, bf16[1,512,512]{2,1,0:T(8,128)(2,1)S(1)}, u32[]{:S(2)}, u32[]{:S(2)}) collective-permute-start(bf16[1,512,512]{2,1,0:T(8,128)(2,1)S(1)} %get-tuple-element.112), channel_id=1, source_target_pairs={{0,2},{2,0},{4,6},{6,4},{8,10},{10,8},{12,14},{14,12},{1,3},{3,1},... | collective-permute-start | bytes 1572872 | tf_op jit(solution)/shard_map/ppermute | solution.py:438
  89.4 0.7 shard_map.189
  90.1 1.7 collective-permute-start.21
  91.8 0.7 shard_map.191
  92.5 1.1 collective-permute-start.24
  93.6 0.8 collective-permute-start.8
  94.4 0.7 shard_map.193
  95.1 1.5 collective-permute-start.27
  96.6 8.3 %collective-permute-done.21.got_ref = bf16[1,256,512]{2,1,0:T(8,128)(2,1)S(1)} collective-permute-done((bf16[1,256,512]{2,1,0:T(8,128)(2,1)S(1)}, bf16[1,256,512]{2,1,0:T(8,128)(2,1)S(1)}, u32[]{:S(2)}, u32[]{:S(2)}) %collective-permute-start.21) | collective-permute-done | bytes 262176 | tf_op jit(solution)/shard_map/ppermute | solution.py:438
  104.9 0.6 shard_map.190
  105.6 1.8 %shard_map.178.own_ref = bf16[512,1024]{1,0:T(8,128)(2,1)S(1)} custom-call(bf16[1,512,512]{2,1,0:T(8,128)(2,1)S(1)} %get-tuple-element.95.refs_2_.q_ref, bf16[2,512,512]{2,1,0:T(8,128)(2,1)S(1)} %get-tuple-element.102.kv_ref, bf16[3,1024,512]{2,1,0:T(8,128)(2,1)S(1)} %bitcast.33), custom_call_target="tpu_custom_call" | custom-call | tf_op jit(solution)/shard_map/pallas_call | solution.py:674
  107.5 2.5 %collective-permute-done.27.got_ref = bf16[1,256,512]{2,1,0:T(8,128)(2,1)S(1)} collective-permute-done((bf16[1,256,512]{2,1,0:T(8,128)(2,1)S(1)}, bf16[1,256,512]{2,1,0:T(8,128)(2,1)S(1)}, u32[]{:S(2)}, u32[]{:S(2)}) %collective-permute-start.27) | collective-permute-done | bytes 262176 | tf_op jit(solution)/shard_map/ppermute | solution.py:438
  110.1 1.7 collective-permute-start.14
  111.7 0.6 collective-permute-done.22
  112.3 0.6 shard_map.192
  113.0 0.6 shard_map.194
  113.7 0.7 shard_map.182
  114.4 11.7 %collective-permute-done.25 = bf16[1,128,512]{2,1,0:T(8,128)(2,1)S(1)} collective-permute-done((bf16[1,128,512]{2,1,0:T(8,128)(2,1)S(1)}, bf16[1,128,512]{2,1,0:T(8,128)(2,1)S(1)}, u32[]{:S(2)}, u32[]{:S(2)}) %collective-permute-start.25) | collective-permute-done | bytes 131104 | tf_op jit(solution)/shard_map/ppermute | solution.py:438
  126.1 1.9 %collective-permute-start.12 = (bf16[1,256,512]{2,1,0:T(8,128)(2,1)S(1)}, bf16[1,256,512]{2,1,0:T(8,128)(2,1)S(1)}, u32[]{:S(2)}, u32[]{:S(2)}) collective-permute-start(bf16[1,256,512]{2,1,0:T(8,128)(2,1)S(1)} %get-tuple-element.114), channel_id=1, source_target_pairs={{0,4},{2,6},{4,0},{6,2},{8,12},{10,14},{12,8},{14,10},{1,5},{3,7},... | collective-permute-start | bytes 786440 | tf_op jit(solution)/shard_map/ppermute | solution.py:438
  128.0 1.6 collective-permute-start.28
  129.7 1.4 shard_map.184
  131.1 4.9 %collective-permute-done.12.got_ref = bf16[1,256,512]{2,1,0:T(8,128)(2,1)S(1)} collective-permute-done((bf16[1,256,512]{2,1,0:T(8,128)(2,1)S(1)}, bf16[1,256,512]{2,1,0:T(8,128)(2,1)S(1)}, u32[]{:S(2)}, u32[]{:S(2)}) %collective-permute-start.12) | collective-permute-done | bytes 262176 | tf_op jit(solution)/shard_map/ppermute | solution.py:438
  136.0 1.7 collective-permute-start.15
  137.7 1.3 shard_map.183
  139.0 1.2 collective-permute-start.13
  140.2 1.6 shard_map.180
  142.2 0.7 add_bitcast_fusion
  142.9 3.5 %shard_map.179 = (bf16[512,1024]{1,0:T(8,128)(2,1)}, f32[1,64,128]{2,1,0:T(8,128)}, f32[1,64,128]{2,1,0:T(8,128)S(1)}) custom-call(s32[2]{0:T(128)S(1)} %pad_add_fusion.place_ref, bf16[512,1024]{1,0:T(8,128)(2,1)S(1)} %copy-done.1, f32[512,1]{1,0:T(8,128)S(1)} %get-tuple-element.87.center_ref, f32[512,1]{1,0:T(8,128)S(1)} %get-tuple-element.88.inverse_ref, ...), custom_call_target="tpu_custom_call" | custom-call | tf_op jit(solution)/shard_map/pallas_call | solution.py:676
  146.5 0.6 copy-done.9
  147.1 1.4 collective-permute-start.17
  148.5 1.2 copy.21
  149.7 1.8 %copy.22 = f32[512,128]{1,0:T(8,128)} copy(f32[512,128]{0,1:T(8,128)} %add_bitcast_fusion) | data formatting | bytes 524288
  151.4 2.6 %shard_map.174 = bf16[512,1024]{1,0:T(8,128)(2,1)} custom-call(f32[512,1024]{1,0:T(8,128)S(1)} %get-tuple-element.85.hidden_ref.source_ref, bf16[512,1024]{1,0:T(8,128)(2,1)S(1)} %get-tuple-element.86.own_ref, bf16[512,1024]{1,0:T(8,128)(2,1)} %collective-permute-done.3.other_ref), custom_call_target="tpu_custom_call" | custom-call | tf_op jit(solution)/shard_map/pallas_call | solution.py:689
  154.0 1.0 shard_map.185
  155.1 0.7 collective-permute-start.16
  155.8 0.8 shard_map.186
  156.6 1.7 collective-permute-start.18
  158.4 0.9 convert_add_fusion.2
  159.3 1.1 collective-permute-done.18.got_ref
  160.4 0.6 shard_map.187
  161.0 3.0 %collective-permute-start.19 = (f32[1,16,128]{2,1,0:T(8,128)S(1)}, f32[1,16,128]{2,1,0:T(8,128)S(1)}, u32[]{:S(2)}, u32[]{:S(2)}) collective-permute-start(f32[1,16,128]{2,1,0:T(8,128)S(1)} %get-tuple-element.129), channel_id=1, source_target_pairs={{0,8},{2,10},{4,12},{6,14},{8,0},{10,2},{12,4},{14,6},{1,9},{3,11}... | collective-permute-start | bytes 24584 | tf_op jit(solution)/shard_map/ppermute | solution.py:438
  164.0 1.2 shard_map.181
  165.3 3.2 %collective-permute-done.19 = f32[1,16,128]{2,1,0:T(8,128)S(1)} collective-permute-done((f32[1,16,128]{2,1,0:T(8,128)S(1)}, f32[1,16,128]{2,1,0:T(8,128)S(1)}, u32[]{:S(2)}, u32[]{:S(2)}) %collective-permute-start.19) | collective-permute-done | bytes 8224 | tf_op jit(solution)/shard_map/ppermute | solution.py:438
  169.0 6.2 %collective-permute-done.10 = bf16[2,128,512]{2,1,0:T(8,128)(2,1)S(1)} collective-permute-done((bf16[2,128,512]{2,1,0:T(8,128)(2,1)S(1)}, bf16[2,128,512]{2,1,0:T(8,128)(2,1)S(1)}, u32[]{:S(2)}, u32[]{:S(2)}) %collective-permute-start.10) | collective-permute-done | bytes 262176 | tf_op jit(solution)/shard_map/ppermute | solution.py:438
  175.4 0.8 copy.20
  176.2 0.9 maximum_bitcast_fusion
  (66 shorter events, 2.5 us)
Async XLA Ops:
  0.6 15.4 %copy-start.13 = (bf16[1024,2,512]{2,1,0:T(2,128)(2,1)S(1)}, bf16[1024,2,512]{2,1,0:T(2,128)(2,1)}, u32[]{:S(2)}) copy-start(bf16[1024,2,512]{2,1,0:T(2,128)(2,1)} %param.15) | copy-start | bytes 6291460
  0.7 15.7 %copy-start.7 = (f32[1024]{0:T(1024)S(1)}, f32[1024]{0:T(1024)}, u32[]{:S(2)}) copy-start(f32[1024]{0:T(1024)} %param.14) | copy-start | bytes 12292
  2.3 14.1 %copy-start = (bf16[1024,3,512]{2,0,1:T(8,128)(2,1)S(1)}, bf16[1024,3,512]{2,0,1:T(8,128)(2,1)}, u32[]{:S(2)}) copy-start(bf16[1024,3,512]{2,0,1:T(8,128)(2,1)} %param.12) | copy-start | bytes 9437188
  2.3 14.1 %copy-start.1 = (bf16[512,1024]{1,0:T(8,128)(2,1)S(1)}, bf16[512,1024]{1,0:T(8,128)(2,1)}, u32[]{:S(2)}) copy-start(bf16[512,1024]{1,0:T(8,128)(2,1)} %source_ref.1) | copy-start | bytes 3145732
  2.3 13.7 %collective-permute-start = (bf16[176,1024]{1,0:T(8,128)(2,1)S(1)}, bf16[176,1024]{1,0:T(8,128)(2,1)S(1)}, u32[]{:S(2)}, u32[]{:S(2)}) collective-permute-start(bf16[176,1024]{1,0:T(8,128)(2,1)S(1)} %shard_map.169), channel_id=1, source_target_pairs={{0,2},{2,4},{4,6},{6,8},{8,10},{10,12},{12,14},{3,1},{5,3},{7,5},{... | collective-permute-start | bytes 1081352 | tf_op jit(solution)/shard_map/ppermute | solution.py:481
  16.1 3.6 %collective-permute-start.1 = (bf16[176,1024]{1,0:T(8,128)(2,1)S(1)}, bf16[176,1024]{1,0:T(8,128)(2,1)S(1)}, u32[]{:S(2)}, u32[]{:S(2)}) collective-permute-start(bf16[176,1024]{1,0:T(8,128)(2,1)S(1)} %collective-permute-done.mine_ref), channel_id=1, source_target_pairs={{0,1},{1,0},{2,3},{3,2},{4,5},{5,4},{6,7},{7,6},{8,9},{9,8},{10,11... | collective-permute-start | bytes 1081352 | tf_op jit(solution)/shard_map/ppermute | solution.py:485
  19.6 3.3 %copy-start.3 = (bf16[512,1024]{1,0:T(8,128)(2,1)S(1)}, bf16[512,1024]{1,0:T(8,128)(2,1)}, u32[]{:S(2)}) copy-start(bf16[512,1024]{1,0:T(8,128)(2,1)} %w_ref.3) | copy-start | bytes 3145732
  19.6 3.3 %copy-start.12 = (s32[512]{0:T(512)S(1)}, s32[512]{0:T(512)}, u32[]{:S(2)}) copy-start(s32[512]{0:T(512)} %param.11) | copy-start | bytes 6148
  22.9 7.9 %copy-start.2 = (bf16[512,1024]{1,0:T(8,128)(2,1)S(1)}, bf16[512,1024]{1,0:T(8,128)(2,1)}, u32[]{:S(2)}) copy-start(bf16[512,1024]{1,0:T(8,128)(2,1)} %refs_0_.1) | copy-start | bytes 3145732
  22.9 7.9 %copy-start.4 = (bf16[512,1024]{1,0:T(8,128)(2,1)S(1)}, bf16[512,1024]{1,0:T(8,128)(2,1)}, u32[]{:S(2)}) copy-start(bf16[512,1024]{1,0:T(8,128)(2,1)} %w_out_ref.1) | copy-start | bytes 3145732
  22.9 7.9 %copy-start.8 = (f32[9,512]{1,0:T(8,128)S(1)}, f32[9,512]{1,0:T(8,128)}, u32[]{:S(2)}) copy-start(f32[9,512]{1,0:T(8,128)} %taps_ref.1) | copy-start | bytes 55300
  22.9 7.9 %copy-start.11 = (f32[1024]{0:T(1024)S(1)}, f32[1024]{0:T(1024)}, u32[]{:S(2)}) copy-start(f32[1024]{0:T(1024)} %param.17) | copy-start | bytes 12292
  27.9 3.0 %collective-permute-start.2 = (bf16[544,1024]{1,0:T(8,128)(2,1)S(1)}, bf16[544,1024]{1,0:T(8,128)(2,1)S(1)}, u32[]{:S(2)}, u32[]{:S(2)}) collective-permute-start(bf16[544,1024]{1,0:T(8,128)(2,1)S(1)} %get-tuple-element.82.own_ref), channel_id=1, source_target_pairs={{0,1},{1,0},{2,3},{3,2},{4,5},{5,4},{6,7},{7,6},{8,9},{9,8},{10,11... | collective-permute-start | bytes 3342344 | tf_op jit(solution)/shard_map/ppermute | solution.py:485
  43.2 7.6 %collective-permute-start.4 = (bf16[512,1024]{1,0:T(8,128)(2,1)S(1)}, bf16[512,1024]{1,0:T(8,128)(2,1)S(1)}, u32[]{:S(2)}, u32[]{:S(2)}) collective-permute-start(bf16[512,1024]{1,0:T(8,128)(2,1)S(1)} %get-tuple-element.91.own_ref), channel_id=1, source_target_pairs={{0,1},{1,0},{2,3},{3,2},{4,5},{5,4},{6,7},{7,6},{8,9},{9,8},{10,11... | collective-permute-start | bytes 3145736 | tf_op jit(solution)/shard_map/ppermute | solution.py:485
  46.6 42.8 %collective-permute-start.20 = (bf16[1,512,512]{2,1,0:T(8,128)(2,1)S(1)}, bf16[1,512,512]{2,1,0:T(8,128)(2,1)S(1)}, u32[]{:S(2)}, u32[]{:S(2)}) collective-permute-start(bf16[1,512,512]{2,1,0:T(8,128)(2,1)S(1)} %get-tuple-element.133), channel_id=1, source_target_pairs={{0,2},{2,0},{4,6},{6,4},{8,10},{10,8},{12,14},{14,12},{1,3},{3,1},... | collective-permute-start | bytes 1572872 | tf_op jit(solution)/shard_map/ppermute | solution.py:438
  49.1 42.7 %collective-permute-start.23 = (bf16[1,512,512]{2,1,0:T(8,128)(2,1)S(1)}, bf16[1,512,512]{2,1,0:T(8,128)(2,1)S(1)}, u32[]{:S(2)}, u32[]{:S(2)}) collective-permute-start(bf16[1,512,512]{2,1,0:T(8,128)(2,1)S(1)} %get-tuple-element.139), channel_id=1, source_target_pairs={{0,4},{2,6},{4,0},{6,2},{8,12},{10,14},{12,8},{14,10},{1,5},{3,7},... | collective-permute-start | bytes 1572872 | tf_op jit(solution)/shard_map/ppermute | solution.py:438
  50.7 43.7 %collective-permute-start.26 = (bf16[1,512,512]{2,1,0:T(8,128)(2,1)S(1)}, bf16[1,512,512]{2,1,0:T(8,128)(2,1)S(1)}, u32[]{:S(2)}, u32[]{:S(2)}) collective-permute-start(bf16[1,512,512]{2,1,0:T(8,128)(2,1)S(1)} %get-tuple-element.145), channel_id=1, source_target_pairs={{0,2},{2,0},{4,6},{6,4},{8,10},{10,8},{12,14},{14,12},{1,3},{3,1},... | collective-permute-start | bytes 1572872 | tf_op jit(solution)/shard_map/ppermute | solution.py:438
  59.4 23.7 %collective-permute-start.5 = (bf16[2,128,512]{2,1,0:T(8,128)(2,1)S(1)}, bf16[2,128,512]{2,1,0:T(8,128)(2,1)S(1)}, u32[]{:S(2)}, u32[]{:S(2)}) collective-permute-start(bf16[2,128,512]{2,1,0:T(8,128)(2,1)S(1)} %get-tuple-element.100), channel_id=1, source_target_pairs={{0,2},{2,4},{4,6},{6,8},{8,10},{10,12},{12,14},{1,3},{3,5},{5,7},{... | collective-permute-start | bytes 786440 | tf_op jit(solution)/shard_map/ppermute | solution.py:492
  63.3 19.8 %collective-permute-start.6 = (bf16[2,128,512]{2,1,0:T(8,128)(2,1)S(1)}, bf16[2,128,512]{2,1,0:T(8,128)(2,1)S(1)}, u32[]{:S(2)}, u32[]{:S(2)}) collective-permute-start(bf16[2,128,512]{2,1,0:T(8,128)(2,1)S(1)} %get-tuple-element.101), channel_id=1, source_target_pairs={{2,0},{4,2},{6,4},{8,6},{10,8},{12,10},{14,12},{3,1},{5,3},{7,5},{... | collective-permute-start | bytes 786440 | tf_op jit(solution)/shard_map/ppermute | solution.py:493
  86.9 26.1 %collective-permute-start.11 = (bf16[1,512,512]{2,1,0:T(8,128)(2,1)S(1)}, bf16[1,512,512]{2,1,0:T(8,128)(2,1)S(1)}, u32[]{:S(2)}, u32[]{:S(2)}) collective-permute-start(bf16[1,512,512]{2,1,0:T(8,128)(2,1)S(1)} %get-tuple-element.112), channel_id=1, source_target_pairs={{0,2},{2,0},{4,6},{6,4},{8,10},{10,8},{12,14},{14,12},{1,3},{3,1},... | collective-permute-start | bytes 1572872 | tf_op jit(solution)/shard_map/ppermute | solution.py:438
  90.1 14.7 %collective-permute-start.21 = (bf16[1,256,512]{2,1,0:T(8,128)(2,1)S(1)}, bf16[1,256,512]{2,1,0:T(8,128)(2,1)S(1)}, u32[]{:S(2)}, u32[]{:S(2)}) collective-permute-start(bf16[1,256,512]{2,1,0:T(8,128)(2,1)S(1)} %get-tuple-element.135), channel_id=1, source_target_pairs={{0,4},{2,6},{4,0},{6,2},{8,12},{10,14},{12,8},{14,10},{1,5},{3,7},... | collective-permute-start | bytes 786440 | tf_op jit(solution)/shard_map/ppermute | solution.py:438
  92.5 14.9 %collective-permute-start.24 = (bf16[1,256,512]{2,1,0:T(8,128)(2,1)S(1)}, bf16[1,256,512]{2,1,0:T(8,128)(2,1)S(1)}, u32[]{:S(2)}, u32[]{:S(2)}) collective-permute-start(bf16[1,256,512]{2,1,0:T(8,128)(2,1)S(1)} %get-tuple-element.141), channel_id=1, source_target_pairs={{0,8},{2,10},{4,12},{6,14},{8,0},{10,2},{12,4},{14,6},{1,9},{3,11}... | collective-permute-start | bytes 786440 | tf_op jit(solution)/shard_map/ppermute | solution.py:438
  93.6 45.4 %collective-permute-start.8 = (bf16[2,512,512]{2,1,0:T(8,128)(2,1)S(1)}, bf16[2,512,512]{2,1,0:T(8,128)(2,1)S(1)}, u32[]{:S(2)}, u32[]{:S(2)}) collective-permute-start(bf16[2,512,512]{2,1,0:T(8,128)(2,1)S(1)} %get-tuple-element.106), channel_id=1, source_target_pairs={{0,2},{2,0},{4,6},{6,4},{8,10},{10,8},{12,14},{14,12},{1,3},{3,1},... | collective-permute-start | bytes 3145736 | tf_op jit(solution)/shard_map/ppermute | solution.py:438
  95.1 14.9 %collective-permute-start.27 = (bf16[1,256,512]{2,1,0:T(8,128)(2,1)S(1)}, bf16[1,256,512]{2,1,0:T(8,128)(2,1)S(1)}, u32[]{:S(2)}, u32[]{:S(2)}) collective-permute-start(bf16[1,256,512]{2,1,0:T(8,128)(2,1)S(1)} %get-tuple-element.147), channel_id=1, source_target_pairs={{0,4},{2,6},{4,0},{6,2},{8,12},{10,14},{12,8},{14,10},{1,5},{3,7},... | collective-permute-start | bytes 786440 | tf_op jit(solution)/shard_map/ppermute | solution.py:438
  105.5 6.8 %collective-permute-start.22 = (bf16[1,128,512]{2,1,0:T(8,128)(2,1)S(1)}, bf16[1,128,512]{2,1,0:T(8,128)(2,1)S(1)}, u32[]{:S(2)}, u32[]{:S(2)}) collective-permute-start(bf16[1,128,512]{2,1,0:T(8,128)(2,1)S(1)} %get-tuple-element.138), channel_id=1, source_target_pairs={{0,8},{2,10},{4,12},{6,14},{8,0},{10,2},{12,4},{14,6},{1,9},{3,11}... | collective-permute-start | bytes 393224 | tf_op jit(solution)/shard_map/ppermute | solution.py:438
  107.4 35.5 %collective-permute-start.7 = (bf16[512,1024]{1,0:T(8,128)(2,1)S(1)}, bf16[512,1024]{1,0:T(8,128)(2,1)S(1)}, u32[]{:S(2)}, u32[]{:S(2)}) collective-permute-start(bf16[512,1024]{1,0:T(8,128)(2,1)S(1)} %shard_map.178.own_ref), channel_id=1, source_target_pairs={{0,1},{1,0},{2,3},{3,2},{4,5},{5,4},{6,7},{7,6},{8,9},{9,8},{10,11... | collective-permute-start | bytes 3145736 | tf_op jit(solution)/shard_map/ppermute | solution.py:485
  110.1 17.9 %collective-permute-start.14 = (bf16[1,512,512]{2,1,0:T(8,128)(2,1)S(1)}, bf16[1,512,512]{2,1,0:T(8,128)(2,1)S(1)}, u32[]{:S(2)}, u32[]{:S(2)}) collective-permute-start(bf16[1,512,512]{2,1,0:T(8,128)(2,1)S(1)} %get-tuple-element.118), channel_id=1, source_target_pairs={{0,4},{2,6},{4,0},{6,2},{8,12},{10,14},{12,8},{14,10},{1,5},{3,7},... | collective-permute-start | bytes 1572872 | tf_op jit(solution)/shard_map/ppermute | solution.py:438
  112.3 39.2 %collective-permute-start.3 = (bf16[512,1024]{1,0:T(8,128)(2,1)S(1)}, bf16[512,1024]{1,0:T(8,128)(2,1)}, u32[]{:S(2)}, u32[]{:S(2)}) collective-permute-start(bf16[512,1024]{1,0:T(8,128)(2,1)S(1)} %get-tuple-element.86.own_ref), channel_id=1, source_target_pairs={{0,1},{1,0},{2,3},{3,2},{4,5},{5,4},{6,7},{7,6},{8,9},{9,8},{10,11... | collective-permute-start | bytes 3145736 | tf_op jit(solution)/shard_map/ppermute | solution.py:485
  112.9 13.2 %collective-permute-start.25 = (bf16[1,128,512]{2,1,0:T(8,128)(2,1)S(1)}, bf16[1,128,512]{2,1,0:T(8,128)(2,1)S(1)}, u32[]{:S(2)}, u32[]{:S(2)}) collective-permute-start(bf16[1,128,512]{2,1,0:T(8,128)(2,1)S(1)} %get-tuple-element.144), channel_id=1, source_target_pairs={{0,2},{2,0},{4,6},{6,4},{8,10},{10,8},{12,14},{14,12},{1,3},{3,1},... | collective-permute-start | bytes 393224 | tf_op jit(solution)/shard_map/ppermute | solution.py:438
  126.1 9.9 %collective-permute-start.12 = (bf16[1,256,512]{2,1,0:T(8,128)(2,1)S(1)}, bf16[1,256,512]{2,1,0:T(8,128)(2,1)S(1)}, u32[]{:S(2)}, u32[]{:S(2)}) collective-permute-start(bf16[1,256,512]{2,1,0:T(8,128)(2,1)S(1)} %get-tuple-element.114), channel_id=1, source_target_pairs={{0,4},{2,6},{4,0},{6,2},{8,12},{10,14},{12,8},{14,10},{1,5},{3,7},... | collective-permute-start | bytes 786440 | tf_op jit(solution)/shard_map/ppermute | solution.py:438
  128.0 13.8 %collective-permute-start.28 = (bf16[1,128,512]{2,1,0:T(8,128)(2,1)S(1)}, bf16[1,128,512]{2,1,0:T(8,128)(2,1)S(1)}, u32[]{:S(2)}, u32[]{:S(2)}) collective-permute-start(bf16[1,128,512]{2,1,0:T(8,128)(2,1)S(1)} %get-tuple-element.150), channel_id=1, source_target_pairs={{0,8},{2,10},{4,12},{6,14},{8,0},{10,2},{12,4},{14,6},{1,9},{3,11}... | collective-permute-start | bytes 393224 | tf_op jit(solution)/shard_map/ppermute | solution.py:438
  136.0 18.0 %collective-permute-start.15 = (bf16[1,256,512]{2,1,0:T(8,128)(2,1)}, bf16[1,256,512]{2,1,0:T(8,128)(2,1)}, u32[]{:S(2)}, u32[]{:S(2)}) collective-permute-start(bf16[1,256,512]{2,1,0:T(8,128)(2,1)} %get-tuple-element.120), channel_id=1, source_target_pairs={{0,8},{2,10},{4,12},{6,14},{8,0},{10,2},{12,4},{14,6},{1,9},{3,11}... | collective-permute-start | bytes 786440 | tf_op jit(solution)/shard_map/ppermute | solution.py:438
  139.0 19.4 %collective-permute-start.13 = (bf16[1,128,512]{2,1,0:T(8,128)(2,1)}, bf16[1,128,512]{2,1,0:T(8,128)(2,1)}, u32[]{:S(2)}, u32[]{:S(2)}) collective-permute-start(bf16[1,128,512]{2,1,0:T(8,128)(2,1)} %get-tuple-element.117), channel_id=1, source_target_pairs={{0,8},{2,10},{4,12},{6,14},{8,0},{10,2},{12,4},{14,6},{1,9},{3,11}... | collective-permute-start | bytes 393224 | tf_op jit(solution)/shard_map/ppermute | solution.py:438
  141.8 4.6 %copy-start.5 = (bf16[2,256,512]{2,1,0:T(8,128)(2,1)}, bf16[2,256,512]{2,1,0:T(8,128)(2,1)S(1)}, u32[]{:S(2)}) copy-start(bf16[2,256,512]{2,1,0:T(8,128)(2,1)S(1)} %get-tuple-element.109.kept_ref) | copy-start | bytes 1572868
  141.8 22.1 %collective-permute-start.9 = (bf16[2,256,512]{2,1,0:T(8,128)(2,1)}, bf16[2,256,512]{2,1,0:T(8,128)(2,1)}, u32[]{:S(2)}, u32[]{:S(2)}) collective-permute-start(bf16[2,256,512]{2,1,0:T(8,128)(2,1)} %get-tuple-element.108), channel_id=1, source_target_pairs={{0,4},{2,6},{4,0},{6,2},{8,12},{10,14},{12,8},{14,10},{1,5},{3,7},... | collective-permute-start | bytes 1572872 | tf_op jit(solution)/shard_map/ppermute | solution.py:438
  146.4 0.6 copy-start.9
  147.1 8.7 %collective-permute-start.17 = (f32[1,64,128]{2,1,0:T(8,128)}, f32[1,64,128]{2,1,0:T(8,128)}, u32[]{:S(2)}, u32[]{:S(2)}) collective-permute-start(f32[1,64,128]{2,1,0:T(8,128)} %get-tuple-element.124), channel_id=1, source_target_pairs={{0,2},{2,0},{4,6},{6,4},{8,10},{10,8},{12,14},{14,12},{1,3},{3,1},... | collective-permute-start | bytes 98312 | tf_op jit(solution)/shard_map/ppermute | solution.py:438
  151.4 4.4 %copy-start.10 = (f32[1,64,128]{2,1,0:T(8,128)S(1)}, f32[1,64,128]{2,1,0:T(8,128)}, u32[]{:S(2)}) copy-start(f32[1,64,128]{2,1,0:T(8,128)} %copy-done.9) | copy-start | bytes 98308
  151.4 12.5 %copy-start.6 = (bf16[2,256,512]{2,1,0:T(8,128)(2,1)S(1)}, bf16[2,256,512]{2,1,0:T(8,128)(2,1)}, u32[]{:S(2)}) copy-start(bf16[2,256,512]{2,1,0:T(8,128)(2,1)} %copy-done.5) | copy-start | bytes 1572868
  155.1 10.2 %collective-permute-start.16 = (bf16[1,128,512]{2,1,0:T(8,128)(2,1)S(1)}, bf16[1,128,512]{2,1,0:T(8,128)(2,1)S(1)}, u32[]{:S(2)}, u32[]{:S(2)}) collective-permute-start(bf16[1,128,512]{2,1,0:T(8,128)(2,1)S(1)} %get-tuple-element.123), channel_id=1, source_target_pairs={{0,2},{2,0},{4,6},{6,4},{8,10},{10,8},{12,14},{14,12},{1,3},{3,1},... | collective-permute-start | bytes 393224 | tf_op jit(solution)/shard_map/ppermute | solution.py:438
  156.6 3.8 %collective-permute-start.18 = (f32[1,32,128]{2,1,0:T(8,128)S(1)}, f32[1,32,128]{2,1,0:T(8,128)S(1)}, u32[]{:S(2)}, u32[]{:S(2)}) collective-permute-start(f32[1,32,128]{2,1,0:T(8,128)S(1)} %get-tuple-element.126), channel_id=1, source_target_pairs={{0,4},{2,6},{4,0},{6,2},{8,12},{10,14},{12,8},{14,10},{1,5},{3,7},... | collective-permute-start | bytes 49160 | tf_op jit(solution)/shard_map/ppermute | solution.py:438
  161.0 7.5 %collective-permute-start.19 = (f32[1,16,128]{2,1,0:T(8,128)S(1)}, f32[1,16,128]{2,1,0:T(8,128)S(1)}, u32[]{:S(2)}, u32[]{:S(2)}) collective-permute-start(f32[1,16,128]{2,1,0:T(8,128)S(1)} %get-tuple-element.129), channel_id=1, source_target_pairs={{0,8},{2,10},{4,12},{6,14},{8,0},{10,2},{12,4},{14,6},{1,9},{3,11}... | collective-permute-start | bytes 24584 | tf_op jit(solution)/shard_map/ppermute | solution.py:438
  165.2 10.1 %collective-permute-start.10 = (bf16[2,128,512]{2,1,0:T(8,128)(2,1)S(1)}, bf16[2,128,512]{2,1,0:T(8,128)(2,1)S(1)}, u32[]{:S(2)}, u32[]{:S(2)}) collective-permute-start(bf16[2,128,512]{2,1,0:T(8,128)(2,1)S(1)} %get-tuple-element.111), channel_id=1, source_target_pairs={{0,8},{2,10},{4,12},{6,14},{8,0},{10,2},{12,4},{14,6},{1,9},{3,11}... | collective-permute-start | bytes 786440 | tf_op jit(solution)/shard_map/ppermute | solution.py:438
  168.5 8.6 %copy-start.14 = (f32[1,16,128]{2,1,0:T(8,128)}, f32[1,16,128]{2,1,0:T(8,128)S(1)}, u32[]{:S(2)}) copy-start(f32[1,16,128]{2,1,0:T(8,128)S(1)} %add.24) | copy-start | bytes 24580
